TPU v7x, 32 devices: a whole 2x2x4 slice. The times are simulated.
32 devices in a mesh: shard: 2 (over y), ctx: 4 (over x, core), tp: 4 (over z).
Axes of the slice: x: 2, y: 2, z: 4, core: 2. Of those that a mesh axis runs over, the one named last changes fastest.
Arguments:
- image_tokens: bfloat16 [4, 1024, 1536], P('shard', 'ctx', 'tp'), may hold values from -6 to 6
- text_tokens: bfloat16 [4, 256, 1536], P('shard', 'ctx', 'tp'), may hold values from -6 to 6
- conditioning: bfloat16 [4, 1536], replicated, may hold values from -16 to 16
- seq_table: int32 [4], replicated, may hold values from 0 to 3, each once
- image_len: int32 [4], replicated, may hold values from 256 to 1024, as said below
- text_len: int32 [4], replicated, may hold values from 38 to 154, as said below
- mod_weight: bfloat16 [2, 1536, 6, 1536], P(None, ('shard', 'ctx', 'tp')), may hold values from -0.15625 to 0.15625
- mod_bias: bfloat16 [2, 6, 1536], P(None, None, ('shard', 'ctx', 'tp')), may hold values from -3 to 3
- qkv_weight: bfloat16 [2, 1536, 3, 1536], P(None, ('shard', 'ctx'), None, 'tp'), may hold values from -0.15625 to 0.15625
- qkv_bias: bfloat16 [2, 2, 24, 64], P(None, None, 'tp', ('shard', 'ctx')), may hold values from -1.1953125 to 1.1953125
- out_weight: bfloat16 [2, 1536, 1536], P(None, ('shard', 'ctx'), 'tp'), may hold values from -0.75 to 0.75
- out_bias: bfloat16 [2, 24, 64], P(None, 'tp', ('shard', 'ctx')), may hold values from -3 to 3
- fc1_weight: bfloat16 [2, 1536, 6144], P(None, ('shard', 'ctx'), 'tp'), may hold values from -0.15625 to 0.15625
- fc1_bias: bfloat16 [2, 96, 64], P(None, 'tp', ('shard', 'ctx')), may hold values from -3 to 3
- fc2_weight: bfloat16 [2, 1536, 6144], P(None, ('shard', 'ctx'), 'tp'), may hold values from -0.078125 to 0.078125
- fc2_bias: bfloat16 [2, 24, 64], P(None, 'tp', ('shard', 'ctx')), may hold values from -3 to 3
- image_cot: bfloat16 [4, 1024, 1536], P('shard', 'ctx', 'tp'), may hold values from -6 to 6
- text_cot: bfloat16 [4, 256, 1536], P('shard', 'ctx', 'tp'), may hold values from -6 to 6
Outputs:
- image_out: bfloat16 [4, 1024, 1536], P('shard', 'ctx', 'tp')
- text_out: bfloat16 [4, 256, 1536], P('shard', 'ctx', 'tp')
- image_grad: float32 [4, 1024, 1536], P('shard', 'ctx', 'tp')
- text_grad: float32 [4, 256, 1536], P('shard', 'ctx', 'tp')
- cond_grad: float32 [4, 1536], P(None, ('shard', 'ctx', 'tp'))
- mod_weight_grad: float32 [2, 1536, 6, 1536], P(None, ('shard', 'ctx', 'tp'))
- mod_bias_grad: float32 [2, 6, 1536], P(None, None, ('shard', 'ctx', 'tp'))
- qkv_weight_grad: float32 [2, 1536, 3, 1536], P(None, ('shard', 'ctx'), None, 'tp')
- qkv_bias_grad: float32 [2, 2, 24, 64], P(None, None, 'tp', ('shard', 'ctx'))
- out_weight_grad: float32 [2, 1536, 1536], P(None, ('shard', 'ctx'), 'tp')
- out_bias_grad: float32 [2, 24, 64], P(None, 'tp', ('shard', 'ctx'))
- fc1_weight_grad: float32 [2, 1536, 6144], P(None, ('shard', 'ctx'), 'tp')
- fc1_bias_grad: float32 [2, 96, 64], P(None, 'tp', ('shard', 'ctx'))
- fc2_weight_grad: float32 [2, 1536, 6144], P(None, ('shard', 'ctx'), 'tp')
- fc2_bias_grad: float32 [2, 24, 64], P(None, 'tp', ('shard', 'ctx'))
Inputs may be any that keep to these rules, and one draw needn't show every extreme that they name: Slot s takes conditioning row seq_table[s]; every row is taken once. `image_len`: some slot has all 1024 image tokens valid in every draw. `text_len`: some slot has 154 valid text tokens in every draw; text slots from 154 on are never valid.
All inputs are finite; a program needn't handle non-finite values.
Results may differ from a plain program's by a relative error of at most 0.014.
The roundings to bfloat16 on the way count: a program that leaves them out, or rounds other values in their place, can miss the bound.
Values may be sent and summed in bfloat16 or wider, within the bound.
No kernel may reach another device: no remote copies, remote signals or barrier semaphores. Data moves between devices by JAX's collectives and lax.ppermute only.
A program may use at most 256 MiB of HBM per device.

v0:
```python
from functools import partial
import math

import jax
import jax.numpy as jnp
from jax import lax
from jax.sharding import PartitionSpec as P

HD = 64
LI = 1024
LT = 256
QBLOCK = 640


EPSILON = 1e-06
NEG_LARGE = -1e30
GELU_COEF = math.sqrt(2.0 / math.pi)
PRECISE = lax.Precision.HIGHEST


def as_sent(shard):
    return jax.tree.map(lambda a: a.astype(jnp.bfloat16) if a.dtype == jnp.float32 else a, shard)


def layer_norm(values):
    center = values - jnp.mean(values, -1, keepdims=True)
    inv_std = lax.rsqrt(jnp.mean(center * center, -1, keepdims=True) + EPSILON)
    return (center * inv_std, inv_std)


def norm_back(normed, inv_std, grad_in):
    return inv_std * (
        grad_in
        - jnp.mean(grad_in, -1, keepdims=True)
        - normed * jnp.mean(grad_in * normed, -1, keepdims=True)
    )


def gelu_tanh(values):
    return (
        0.5 * values * (1.0 + jnp.tanh(GELU_COEF * (values + 0.044715 * values * values * values)))
    )


def gelu_slope(values):
    tanh_val = jnp.tanh(GELU_COEF * (values + 0.044715 * values * values * values))
    return 0.5 * (1.0 + tanh_val) + 0.5 * values * (1.0 - tanh_val * tanh_val) * GELU_COEF * (
        1.0 + 0.134145 * values * values
    )


def silu_slope(values):
    sigmoid = jax.nn.sigmoid(values)
    return sigmoid * (1.0 + values * (1.0 - sigmoid))


def full_width(arrays):
    return (
        lax.all_gather(arrays[0], "tp", axis=2, tiled=True),
        lax.all_gather(arrays[1], "tp", axis=2, tiled=True),
    )


def part_sums(arrays):
    return (
        lax.psum_scatter(arrays[0], "tp", scatter_dimension=2, tiled=True),
        lax.psum_scatter(arrays[1], "tp", scatter_dimension=2, tiled=True),
    )


def block_scores(query_block, key_rows, key_valid, score_scale):
    scores = (
        jnp.einsum("qd,kd->qk", query_block, key_rows, preferred_element_type=jnp.float32)
        * score_scale
    )
    return jnp.where(key_valid[None, :], scores, NEG_LARGE)


def head_forward(items, score_scale):
    query_rows, key_rows, value_rows, key_valid = items
    mixed_parts = []
    total_parts = []
    for row_begin in range(0, query_rows.shape[0], QBLOCK):
        scores = block_scores(
            query_rows[row_begin : row_begin + QBLOCK], key_rows, key_valid, score_scale
        )
        top_score = jnp.max(scores, 1, keepdims=True)
        log_total = top_score + jnp.log(jnp.sum(jnp.exp(scores - top_score), 1, keepdims=True))
        weights = jnp.exp(scores - log_total).astype(jnp.bfloat16)
        mixed_parts.append(
            jnp.dot(weights, value_rows, preferred_element_type=jnp.float32).astype(jnp.bfloat16)
        )
        total_parts.append(log_total[:, 0])
    return (jnp.concatenate(mixed_parts, 0), jnp.concatenate(total_parts, 0))


def head_backward(items, score_scale):
    query_rows, key_rows, value_rows, mixed_rows, grad_rows, log_total, key_valid = items
    grad_key = jnp.zeros(key_rows.shape, jnp.float32)
    grad_value = jnp.zeros(value_rows.shape, jnp.float32)
    query_parts = []
    for row_begin in range(0, query_rows.shape[0], QBLOCK):
        finish = row_begin + QBLOCK
        query_block = query_rows[row_begin:finish]
        grad_block = grad_rows[row_begin:finish]
        prob_rows = jnp.exp(
            block_scores(query_block, key_rows, key_valid, score_scale)
            - log_total[row_begin:finish, None]
        )
        grad_prob = jnp.einsum(
            "qd,kd->qk", grad_block, value_rows, preferred_element_type=jnp.float32
        )
        row_delta = jnp.sum(
            grad_block.astype(jnp.float32) * mixed_rows[row_begin:finish].astype(jnp.float32),
            1,
            keepdims=True,
        )
        grad_scores = (prob_rows * (grad_prob - row_delta) * score_scale).astype(jnp.bfloat16)
        query_parts.append(
            jnp.dot(grad_scores, key_rows, preferred_element_type=jnp.float32).astype(jnp.bfloat16)
        )
        grad_key = grad_key + jnp.einsum(
            "qk,qd->kd", grad_scores, query_block, preferred_element_type=jnp.float32
        )
        grad_value = grad_value + jnp.einsum(
            "qk,qd->kd",
            prob_rows.astype(jnp.bfloat16),
            grad_block,
            preferred_element_type=jnp.float32,
        )
    return (
        jnp.concatenate(query_parts, 0),
        grad_key.astype(jnp.bfloat16),
        grad_value.astype(jnp.bfloat16),
    )


def body(
    image_tokens,
    text_tokens,
    conditioning,
    seq_table,
    image_len,
    text_len,
    mod_weight,
    mod_bias,
    qkv_weight,
    qkv_bias,
    out_weight,
    out_bias,
    fc1_weight,
    fc1_bias,
    fc2_weight,
    fc2_bias,
    image_cot,
    text_cot,
):
    group_size = image_tokens.shape[0]
    col_count = image_tokens.shape[2]
    head_local = col_count // HD
    col_begin = lax.axis_index("tp") * col_count
    model_width = conditioning.shape[1]
    row_count = mod_weight.shape[1]
    row_begin = lax.axis_index(("shard", "ctx", "tp")) * row_count
    first_slot = lax.axis_index("shard") * group_size
    score_scale = 1.0 / math.sqrt(HD)

    def to_heads(packed):
        seq_count, tok_count = (packed.shape[0], packed.shape[1])
        shaped = packed.reshape(seq_count, tok_count, 3, head_local, HD)
        return jnp.transpose(shaped, (2, 0, 3, 1, 4)).reshape(
            3, seq_count * head_local, tok_count, HD
        )

    def from_heads(stacked):
        tok_count = stacked.shape[2]
        shaped = stacked.reshape(3, group_size, head_local, tok_count, HD)
        return jnp.transpose(shaped, (1, 3, 0, 2, 4)).reshape(group_size, tok_count, 3, col_count)

    def items_of(rows):
        tok_count = rows.shape[1]
        shaped = rows.reshape(group_size, tok_count, head_local, HD)
        return jnp.transpose(shaped, (0, 2, 1, 3)).reshape(group_size * head_local, tok_count, HD)

    def tokens_of(items):
        tok_count = items.shape[1]
        shaped = items.reshape(group_size, head_local, tok_count, HD)
        return jnp.transpose(shaped, (0, 2, 1, 3)).reshape(group_size, tok_count, col_count)

    cond_rows = jnp.take(conditioning, seq_table, axis=0).astype(jnp.float32)
    cond_act = jax.nn.silu(cond_rows)
    act_part = lax.dynamic_slice_in_dim(cond_act, row_begin, row_count, 1)
    mod_local = mod_weight.astype(jnp.float32)
    mod_term = jnp.einsum("sr,xrke->sxke", act_part, mod_local, precision=PRECISE)
    bias_wide = lax.dynamic_update_slice(
        jnp.zeros(mod_bias.shape[:2] + (model_width,), jnp.float32),
        mod_bias.astype(jnp.float32),
        (0, 0, row_begin),
    )
    mod_all = lax.psum(mod_term + bias_wide[None], ("shard", "ctx", "tp"))
    mod_here = lax.dynamic_slice_in_dim(mod_all, first_slot, group_size, 0)
    gate_cols = lax.dynamic_slice_in_dim(mod_here, col_begin, col_count, 3)
    w_qkv, w_out, w_fc1, w_fc2, b_qkv, b_out, b_fc1, b_fc2 = (
        lax.all_gather(qkv_weight, ("shard", "ctx"), axis=1, tiled=True),
        lax.all_gather(out_weight, ("shard", "ctx"), axis=1, tiled=True),
        lax.all_gather(fc1_weight, ("shard", "ctx"), axis=1, tiled=True),
        lax.all_gather(fc2_weight, ("shard", "ctx"), axis=1, tiled=True),
        lax.all_gather(qkv_bias, ("shard", "ctx"), axis=3, tiled=True),
        lax.all_gather(out_bias, ("shard", "ctx"), axis=2, tiled=True),
        lax.all_gather(fc1_bias, ("shard", "ctx"), axis=2, tiled=True),
        lax.all_gather(fc2_bias, ("shard", "ctx"), axis=2, tiled=True),
    )
    b_qkv = b_qkv.astype(jnp.float32).reshape(2, 2, col_count)
    bias_three = jnp.stack([b_qkv[:, 0], jnp.zeros((2, col_count), jnp.float32), b_qkv[:, 1]], 1)
    b_out = b_out.astype(jnp.float32).reshape(2, col_count)
    b_fc1 = b_fc1.astype(jnp.float32).reshape(2, -1)
    b_fc2 = b_fc2.astype(jnp.float32).reshape(2, col_count)
    inputs = (image_tokens, text_tokens)
    cots = (image_cot, text_cot)
    wide_in = full_width((image_tokens, text_tokens))
    normed_one, inv_one, hidden_one, packed_tok = ([], [], [], [])
    for stream in range(2):
        mod_rows = mod_here[:, stream]
        normed, inv_std = layer_norm(wide_in[stream].astype(jnp.float32))
        hidden = (normed * (1.0 + mod_rows[:, 1, None]) + mod_rows[:, 0, None]).astype(jnp.bfloat16)
        projected = (
            jnp.einsum("snd,dkh->snkh", hidden, w_qkv[stream], preferred_element_type=jnp.float32)
            + bias_three[stream]
        )
        normed_one.append(normed)
        inv_one.append(inv_std)
        hidden_one.append(hidden)
        packed_tok.append(projected.astype(jnp.bfloat16))
    seq_image, seq_text = (
        lax.all_to_all(to_heads(packed_tok[0]), "ctx", split_axis=1, concat_axis=2, tiled=True),
        lax.all_to_all(to_heads(packed_tok[1]), "ctx", split_axis=1, concat_axis=2, tiled=True),
    )
    joint = jnp.concatenate([seq_image, seq_text], 2)
    item_count = joint.shape[1]
    item_ids = lax.axis_index("ctx") * item_count + jnp.arange(item_count, dtype=jnp.int32)
    slots = first_slot + item_ids // head_local
    image_counts = jnp.take(image_len, slots)
    text_counts = jnp.take(text_len, slots)
    masks = jnp.concatenate(
        [
            jnp.arange(LI)[None, :] < image_counts[:, None],
            jnp.arange(LT)[None, :] < text_counts[:, None],
        ],
        1,
    )
    mixed_items, total_items = lax.map(
        partial(head_forward, score_scale=score_scale), (joint[0], joint[1], joint[2], masks)
    )
    mixed_back = (
        lax.all_to_all(
            as_sent(mixed_items[:, :LI]), "ctx", split_axis=1, concat_axis=0, tiled=True
        ),
        lax.all_to_all(
            as_sent(mixed_items[:, LI:]), "ctx", split_axis=1, concat_axis=0, tiled=True
        ),
    )
    mixed_tok = (tokens_of(mixed_back[0]), tokens_of(mixed_back[1]))
    attn_partial = part_sums(
        (
            jnp.einsum("snh,oh->sno", mixed_tok[0], w_out[0], preferred_element_type=jnp.float32),
            jnp.einsum("snh,oh->sno", mixed_tok[1], w_out[1], preferred_element_type=jnp.float32),
        )
    )
    branch_one, resid = ([], [])
    for stream in range(2):
        branch = attn_partial[stream] + b_out[stream]
        branch_one.append(branch)
        resid.append(inputs[stream].astype(jnp.float32) + gate_cols[:, stream, 2, None] * branch)
    wide_resid = (
        lax.all_gather(resid[0], "tp", axis=2, tiled=True),
        lax.all_gather(resid[1], "tp", axis=2, tiled=True),
    )
    normed_two, inv_two, hidden_two, pre_act, act_two, mlp_partial = ([], [], [], [], [], [])
    for stream in range(2):
        mod_rows = mod_here[:, stream]
        normed, inv_std = layer_norm(wide_resid[stream])
        hidden = (normed * (1.0 + mod_rows[:, 4, None]) + mod_rows[:, 3, None]).astype(jnp.bfloat16)
        pre_values = (
            jnp.einsum("snd,df->snf", hidden, w_fc1[stream], preferred_element_type=jnp.float32)
            + b_fc1[stream]
        )
        activated = gelu_tanh(pre_values).astype(jnp.bfloat16)
        normed_two.append(normed)
        inv_two.append(inv_std)
        hidden_two.append(hidden)
        pre_act.append(pre_values)
        act_two.append(activated)
        mlp_partial.append(
            jnp.einsum("snf,of->sno", activated, w_fc2[stream], preferred_element_type=jnp.float32)
        )
    mlp_sums = part_sums((mlp_partial[0], mlp_partial[1]))
    outputs, branch_two = ([], [])
    for stream in range(2):
        branch = mlp_sums[stream] + b_fc2[stream]
        branch_two.append(branch)
        outputs.append(
            (resid[stream] + gate_cols[:, stream, 5, None] * branch).astype(jnp.bfloat16)
        )
    cot_float, grad_two, grad_two_half = ([], [], [])
    for stream in range(2):
        cot_f = cots[stream].astype(jnp.float32)
        grad_values = cot_f * gate_cols[:, stream, 5, None]
        cot_float.append(cot_f)
        grad_two.append(grad_values)
        grad_two_half.append(grad_values.astype(jnp.bfloat16))
    wide_grad_two = full_width((grad_two_half[0], grad_two_half[1]))
    fc2_grads, fc1_grads, fc1_bias_sums, back_two, grad_hidden_two = ([], [], [], [], [])
    for stream in range(2):
        fc2_grads.append(
            jnp.einsum(
                "sno,snf->of",
                wide_grad_two[stream],
                act_two[stream],
                preferred_element_type=jnp.float32,
            )
        )
        grad_act = jnp.einsum(
            "sno,of->snf", wide_grad_two[stream], w_fc2[stream], preferred_element_type=jnp.float32
        ) * gelu_slope(pre_act[stream])
        fc1_bias_sums.append(jnp.sum(grad_act, (0, 1)))
        grad_act_half = grad_act.astype(jnp.bfloat16)
        fc1_grads.append(
            jnp.einsum(
                "snd,snf->df", hidden_two[stream], grad_act_half, preferred_element_type=jnp.float32
            )
        )
        grad_hidden = jnp.einsum(
            "snf,df->snd", grad_act_half, w_fc1[stream], preferred_element_type=jnp.float32
        )
        grad_hidden_two.append(grad_hidden)
        back_two.append(
            norm_back(
                normed_two[stream],
                inv_two[stream],
                grad_hidden * (1.0 + mod_here[:, stream, 4, None]),
            )
        )
    back_two_sums = part_sums((back_two[0], back_two[1]))
    grad_resid, grad_one, grad_one_half = ([], [], [])
    for stream in range(2):
        grad_res = cot_float[stream] + back_two_sums[stream]
        grad_values = grad_res * gate_cols[:, stream, 2, None]
        grad_resid.append(grad_res)
        grad_one.append(grad_values)
        grad_one_half.append(grad_values.astype(jnp.bfloat16))
    wide_grad_one = full_width((grad_one_half[0], grad_one_half[1]))
    out_grads, grad_mixed = ([], [])
    for stream in range(2):
        out_grads.append(
            jnp.einsum(
                "sno,snh->oh",
                wide_grad_one[stream],
                mixed_tok[stream],
                preferred_element_type=jnp.float32,
            )
        )
        grad_mixed.append(
            jnp.einsum(
                "sno,oh->snh",
                wide_grad_one[stream],
                w_out[stream],
                preferred_element_type=jnp.float32,
            ).astype(jnp.bfloat16)
        )
    seq_grad_image, seq_grad_text = (
        lax.all_to_all(items_of(grad_mixed[0]), "ctx", split_axis=0, concat_axis=1, tiled=True),
        lax.all_to_all(items_of(grad_mixed[1]), "ctx", split_axis=0, concat_axis=1, tiled=True),
    )
    grad_joint = jnp.concatenate([seq_grad_image, seq_grad_text], 1)
    grad_query, grad_key, grad_value = lax.map(
        partial(head_backward, score_scale=score_scale),
        (joint[0], joint[1], joint[2], mixed_items, grad_joint, total_items, masks),
    )
    grad_stack = jnp.stack([grad_query, grad_key, grad_value], 0)
    grad_back = (
        lax.all_to_all(
            as_sent(grad_stack[:, :, :LI]), "ctx", split_axis=2, concat_axis=1, tiled=True
        ),
        lax.all_to_all(
            as_sent(grad_stack[:, :, LI:]), "ctx", split_axis=2, concat_axis=1, tiled=True
        ),
    )
    grad_tok = (from_heads(grad_back[0]), from_heads(grad_back[1]))
    qkv_grads, qkv_bias_sums, back_one, grad_hidden_one = ([], [], [], [])
    for stream in range(2):
        qkv_grads.append(
            jnp.einsum(
                "snd,snkh->dkh",
                hidden_one[stream],
                grad_tok[stream],
                preferred_element_type=jnp.float32,
            )
        )
        bias_sum = jnp.sum(grad_tok[stream], (0, 1), dtype=jnp.float32)
        qkv_bias_sums.append(jnp.stack([bias_sum[0], bias_sum[2]], 0))
        grad_hidden = jnp.einsum(
            "snkh,dkh->snd", grad_tok[stream], w_qkv[stream], preferred_element_type=jnp.float32
        )
        grad_hidden_one.append(grad_hidden)
        back_one.append(
            norm_back(
                normed_one[stream],
                inv_one[stream],
                grad_hidden * (1.0 + mod_here[:, stream, 1, None]),
            )
        )
    back_one_sums = part_sums((back_one[0], back_one[1]))
    input_grads = [grad_resid[stream] + back_one_sums[stream] for stream in range(2)]

    def place_cols(values):
        return lax.dynamic_update_slice(
            jnp.zeros((group_size, model_width), jnp.float32), values, (0, col_begin)
        )

    mod_pieces = []
    for stream in range(2):
        mod_pieces.append(
            jnp.stack(
                [
                    jnp.sum(grad_hidden_one[stream], 1),
                    jnp.sum(grad_hidden_one[stream] * normed_one[stream], 1),
                    place_cols(jnp.sum(grad_resid[stream] * branch_one[stream], 1)),
                    jnp.sum(grad_hidden_two[stream], 1),
                    jnp.sum(grad_hidden_two[stream] * normed_two[stream], 1),
                    place_cols(jnp.sum(cot_float[stream] * branch_two[stream], 1)),
                ],
                1,
            )
        )
    mod_place = lax.dynamic_update_slice(
        jnp.zeros(mod_all.shape, jnp.float32), jnp.stack(mod_pieces, 1), (first_slot, 0, 0, 0)
    )
    grad_mod = lax.psum(mod_place, ("shard", "ctx", "tp"))
    mod_weight_grad = jnp.einsum("sr,sxke->xrke", act_part, grad_mod, precision=PRECISE)
    mod_bias_grad = lax.dynamic_slice_in_dim(jnp.sum(grad_mod, 0), row_begin, row_count, 2)
    act_grad = jnp.einsum("sxke,xrke->sr", grad_mod, mod_local, precision=PRECISE)
    slot_grad = act_grad * silu_slope(lax.dynamic_slice_in_dim(cond_rows, row_begin, row_count, 1))
    cond_grad = (
        jnp.zeros((conditioning.shape[0], row_count), jnp.float32).at[seq_table].add(slot_grad)
    )
    grad_terms = (
        jnp.stack(qkv_grads, 0),
        jnp.stack(out_grads, 0),
        jnp.stack(fc1_grads, 0),
        jnp.stack(fc2_grads, 0),
        jnp.stack(qkv_bias_sums, 0).reshape(2, 2, head_local, HD),
        jnp.stack([jnp.sum(grad_one[0], (0, 1)), jnp.sum(grad_one[1], (0, 1))], 0).reshape(
            2, head_local, HD
        ),
        jnp.stack(fc1_bias_sums, 0).reshape(2, -1, HD),
        jnp.stack([jnp.sum(grad_two[0], (0, 1)), jnp.sum(grad_two[1], (0, 1))], 0).reshape(
            2, head_local, HD
        ),
    )
    owned = (
        lax.psum_scatter(grad_terms[0], ("shard", "ctx"), scatter_dimension=1, tiled=True),
        lax.psum_scatter(grad_terms[1], ("shard", "ctx"), scatter_dimension=1, tiled=True),
        lax.psum_scatter(grad_terms[2], ("shard", "ctx"), scatter_dimension=1, tiled=True),
        lax.psum_scatter(grad_terms[3], ("shard", "ctx"), scatter_dimension=1, tiled=True),
        lax.psum_scatter(grad_terms[4], ("shard", "ctx"), scatter_dimension=3, tiled=True),
        lax.psum_scatter(grad_terms[5], ("shard", "ctx"), scatter_dimension=2, tiled=True),
        lax.psum_scatter(grad_terms[6], ("shard", "ctx"), scatter_dimension=2, tiled=True),
        lax.psum_scatter(grad_terms[7], ("shard", "ctx"), scatter_dimension=2, tiled=True),
    )
    (
        qkv_weight_grad,
        out_weight_grad,
        fc1_weight_grad,
        fc2_weight_grad,
        qkv_bias_grad,
        out_bias_grad,
        fc1_bias_grad,
        fc2_bias_grad,
    ) = owned
    return (
        outputs[0],
        outputs[1],
        input_grads[0],
        input_grads[1],
        cond_grad,
        mod_weight_grad,
        mod_bias_grad,
        qkv_weight_grad,
        qkv_bias_grad,
        out_weight_grad,
        out_bias_grad,
        fc1_weight_grad,
        fc1_bias_grad,
        fc2_weight_grad,
        fc2_bias_grad,
    )


def solution(mesh):
    placed = (
        P("shard", "ctx", "tp"),
        P("shard", "ctx", "tp"),
        P(),
        P(),
        P(),
        P(),
        P(None, ("shard", "ctx", "tp"), None, None),
        P(None, None, ("shard", "ctx", "tp")),
        P(None, ("shard", "ctx"), None, "tp"),
        P(None, None, "tp", ("shard", "ctx")),
        P(None, ("shard", "ctx"), "tp"),
        P(None, "tp", ("shard", "ctx")),
        P(None, ("shard", "ctx"), "tp"),
        P(None, "tp", ("shard", "ctx")),
        P(None, ("shard", "ctx"), "tp"),
        P(None, "tp", ("shard", "ctx")),
        P("shard", "ctx", "tp"),
        P("shard", "ctx", "tp"),
    )
    return jax.shard_map(
        body,
        mesh=mesh,
        in_specs=placed,
        out_specs=(
            P("shard", "ctx", "tp"),
            P("shard", "ctx", "tp"),
            P("shard", "ctx", "tp"),
            P("shard", "ctx", "tp"),
            P(None, ("shard", "ctx", "tp")),
            P(None, ("shard", "ctx", "tp"), None, None),
            P(None, None, ("shard", "ctx", "tp")),
            P(None, ("shard", "ctx"), None, "tp"),
            P(None, None, "tp", ("shard", "ctx")),
            P(None, ("shard", "ctx"), "tp"),
            P(None, "tp", ("shard", "ctx")),
            P(None, ("shard", "ctx"), "tp"),
            P(None, "tp", ("shard", "ctx")),
            P(None, ("shard", "ctx"), "tp"),
            P(None, "tp", ("shard", "ctx")),
        ),
        check_vma=False,
    )
```

profile of v0, /device:TPU:0, one launch (start us, length us, event | category | flops | bytes accessed | tf_op | source)
XLA Modules:
  0.0 1511.7 jit_solution(17602792344292564021)
XLA Ops:
  16.8 10.7 all_gather.50
  27.9 20.4 %all_gather.51 = bf16[2,64,1536]{2,1,0:T(8,128)(2,1)S(1)} all-gather(bf16[2,64,384]{2,1,0:T(8,128)(2,1)S(1)} %copy-done.46), channel_id=1, replica_groups=mesh['shard'=2,'ctx'=4,'tp'=4] {'tp'}, dimensions={2}, use_global_device_ids=true | all-gather | bytes 491520 | tf_op jit(solution)/shard_map/all_gather | solution.py:60
  48.7 135.8 %all-reduce.8.cloned.1.call-done = f32[4,2,6,1536]{3,0,2,1:T(4,128)} async-done(((f32[4,2,6,1536]{3,0,2,1:T(4,128)}), f32[4,2,6,1536]{3,0,2,1:T(4,128)}) %all-reduce.8.cloned.1.call-update) | async-done | bytes 294928 | tf_op jit(solution)/shard_map/psum | solution.py:200
  190.6 3.5 fusion.122
  200.7 4.1 all-to-all-start.1
  204.9 5.3 add_convert_fusion.1
  212.8 3.5 all-to-all-start
  221.0 11.1 all-to-all-done
  241.9 22.6 %while.26 = (s32[]{:T(128)}, bf16[3,1280,64]{1,2,0:T(8,128)(2,1)S(1)}, f32[3,1280]{1,0:T(4,128)}, pred[3,1280]{1,0:T(4,128)(4,1)S(1)}, bf16[3,1280,64]{2,1,0:T(8...) while((s32[]{:T(128)}, ...), condition=%wide.region_10.12_spmd, body=%wide.region_5.11_spmd.sunk | while | flops 431308800 | bytes 23835816 | solution.py:251
  271.0 11.6 all_to_all.132
  286.5 4.1 fusion.129
  290.8 9.1 all_gather.53
  303.5 48.6 %reduce-scatter.16.cloned.1.call-done = f32[2,256,384]{2,1,0:T(8,128)} async-done(((f32[2,256,1536]{2,1,0:T(8,128)}), f32[2,256,384]{2,1,0:T(8,128)}) %reduce-scatter.16.cloned.1.call-update) | async-done | bytes 786448 | tf_op jit(solution)/shard_map/reduce_scatter | solution.py:66
  356.5 8.8 all_gather.56
  367.4 3.3 all-to-all-start.3
  378.3 39.2 %all-gather.15.cloned.1.call-done = f32[2,256,1536]{2,1,0:T(8,128)} async-done(((f32[2,256,384]{2,1,0:T(8,128)}), f32[2,256,1536]{2,1,0:T(8,128)}) %all-gather.15.cloned.1.call-update) | async-done | bytes 3145744 | tf_op jit(solution)/shard_map/all_gather | solution.py:275
  422.0 54.7 %all-gather.17.cloned.1.call-done = bf16[2,1536,1536]{2,1,0:T(8,128)(2,1)} async-done(((bf16[2,192,1536]{2,1,0:T(8,128)(2,1)}), bf16[2,1536,1536]{2,1,0:T(8,128)(2,1)}) %all-gather.17.cloned.1.call-update) | async-done | bytes 9437200 | tf_op jit(solution)/shard_map/all_gather | solution.py:206
  476.7 7.6 fusion.93
  484.3 31.0 %all-gather.21.cloned.1.call-done = bf16[2,256,1536]{2,1,0:T(8,128)(2,1)} async-done(((bf16[2,256,384]{2,1,0:T(8,128)(2,1)}), bf16[2,256,1536]{2,1,0:T(8,128)(2,1)}) %all-gather.21.cloned.1.call-update) | async-done | bytes 1572880 | tf_op jit(solution)/shard_map/all_gather | solution.py:59
  515.2 59.6 %all-gather.19.cloned.1.call-done = bf16[2,1536,1536]{2,1,0:T(8,128)(2,1)} async-done(((bf16[2,192,1536]{2,1,0:T(8,128)(2,1)}), bf16[2,1536,1536]{2,1,0:T(8,128)(2,1)}) %all-gather.19.cloned.1.call-update) | async-done | bytes 9437200 | tf_op jit(solution)/shard_map/all_gather | solution.py:207
  574.9 8.5 fusion.191
  583.4 6.4 multiply_reduce_fusion
  592.5 7.7 fusion.74
  601.9 18.8 %all_gather.62 = bf16[2,64,1536]{2,1,0:T(8,128)(2,1)} all-gather(bf16[2,64,384]{2,1,0:T(8,128)(2,1)S(1)} %fusion.159), channel_id=1, replica_groups=mesh['shard'=2,'ctx'=4,'tp'=4] {'tp'}, dimensions={2}, use_global_device_ids=true | all-gather | bytes 491520 | tf_op jit(solution)/shard_map/all_gather | solution.py:60
  622.4 29.5 %all_gather.59 = f32[2,64,1536]{2,1,0:T(8,128)S(1)} all-gather(f32[2,64,384]{2,1,0:T(8,128)S(1)} %multiply_add_fusion.3), channel_id=1, replica_groups=mesh['shard'=2,'ctx'=4,'tp'=4] {'tp'}, dimensions={2}, use_global_device_ids=true | all-gather | bytes 983040 | tf_op jit(solution)/shard_map/all_gather | solution.py:276
  653.6 3.4 fusion.111
  657.1 5.1 fusion.190
  665.8 5.3 fusion.78
  672.6 9.0 all_gather.58
  685.0 56.4 %reduce-scatter.18.cloned.1.call-done = f32[2,256,384]{2,1,0:T(8,128)} async-done(((f32[2,256,1536]{2,1,0:T(8,128)}), f32[2,256,384]{2,1,0:T(8,128)}) %reduce-scatter.18.cloned.1.call-update) | async-done | bytes 786448 | tf_op jit(solution)/shard_map/reduce_scatter | solution.py:66
  741.4 3.6 multiply_reduce_fusion.9
  745.9 21.5 %reduce-scatter.26.cloned.1.call-done = f32[2,64,384]{2,1,0:T(8,128)} async-done(((f32[2,64,1536]{2,1,0:T(8,128)}), f32[2,64,384]{2,1,0:T(8,128)}) %reduce-scatter.26.cloned.1.call-update) | async-done | bytes 196624 | tf_op jit(solution)/shard_map/reduce_scatter | solution.py:67
  767.4 24.9 %reduce-scatter.22.cloned.1.call-done = f32[2,64,384]{2,1,0:T(8,128)} async-done(((f32[2,64,1536]{2,1,0:T(8,128)}), f32[2,64,384]{2,1,0:T(8,128)}) %reduce-scatter.22.cloned.1.call-update) | async-done | bytes 196624 | tf_op jit(solution)/shard_map/reduce_scatter | solution.py:67
  794.9 17.8 %all_gather.63 = bf16[2,64,1536]{2,1,0:T(8,128)(2,1)S(1)} all-gather(bf16[2,64,384]{2,1,0:T(8,128)(2,1)S(1)} %get-tuple-element.370), channel_id=1, replica_groups=mesh['shard'=2,'ctx'=4,'tp'=4] {'tp'}, dimensions={2}, use_global_device_ids=true | all-gather | bytes 491520 | tf_op jit(solution)/shard_map/all_gather | solution.py:60
  816.2 3.3 all-to-all-start.5
  824.3 8.6 all-gather.23.cloned.1.call-done
  836.6 3.7 all-to-all-start.4
  840.9 6.7 all-to-all-done.4
  850.9 89.6 %while.27 = (s32[]{:T(128)}, bf16[3,1280,64]{1,2,0:T(8,128)(2,1)}, bf16[3,1280,64]{1,2,0:T(8,128)(2,1)}, bf16[3,1280,64]{1,2,0:T(8,128)(2,1)}, pred[3,1280]{1,0:...) while((s32[]{:T(128)}, bf16[3,1280,64]{1,2,0:T(8,128)(2,1)}, ...), condition=%wide.region_28.30_spmd, body=%wide.region_25.29_spmd.sunk | while | flops 1062746880 | bytes 67048048 | solution.py:375
  851.8 3.4 fusion.277
  862.4 3.5 fusion.280
  881.7 3.4 fusion.277
  892.3 3.5 fusion.280
  911.6 3.4 fusion.277
  922.2 3.5 fusion.280
  945.1 3.5 all-to-all-start.7
  949.0 3.6 copy.355
  952.5 4.8 reshape.438
  958.1 3.5 all-to-all-start.6
  969.9 4.2 fusion.146
  980.5 5.3 copy.293
  985.9 6.9 fusion.99
  997.1 4.6 fusion.98
  1015.0 6.7 pad_maximum_fusion.1
  1027.5 6.9 pad_maximum_fusion.2
  1035.1 5.3 convolution_bitcast_fusion.4
  1040.4 4.8 convolution_bitcast_fusion.5
  1045.2 11.0 pad_maximum_fusion.3
  1068.2 23.8 %all-reduce.4 = (f32[2,2,6,64]{3,1,2,0:T(2,128)S(1)}, f32[2,6,64]{2,1,0:T(8,128)S(1)}, f32[2,24,64]{1,0,2:T(2,128)S(1)}, f32[2,6,64]{2,1,0:T(8,128)S(1)}) all-reduce(f32[2,2,6,64]{3,1,2,0:T(2,128)S(1)} %copy.306, f32[2,6,64]{2,1,0:T(8,128)S(1)} %pad_maximum_fusion.10, ...), channel_id=11, replica_groups=mesh['shard'=2,'ctx'=4,'tp'=4] {'shard','ctx'}, use_global_device_ids=true, to_apply=%region_53.55.clone | all-reduce | flops 6144 | bytes 49152
  1094.7 69.6 %all-reduce.10.cloned.1.call-done = f32[4,2,6,1536]{3,0,1,2:T(4,128)} async-done(((f32[4,2,6,1536]{3,0,1,2:T(4,128)}), f32[4,2,6,1536]{3,0,1,2:T(4,128)}) %all-reduce.10.cloned.1.call-update) | async-done | bytes 294928 | tf_op jit(solution)/shard_map/psum | solution.py:438
  1169.9 6.4 convolution_bitcast_fusion.6
  1180.1 90.0 %reduce-scatter.36.cloned.1.call-done = f32[2,192,1536]{2,1,0:T(8,128)} async-done(((f32[2,1536,1536]{2,1,0:T(8,128)}), f32[2,192,1536]{2,1,0:T(8,128)}) %reduce-scatter.36.cloned.1.call-update) | async-done | bytes 2359312 | tf_op jit(solution)/shard_map/reduce_scatter | solution.py:463
  1270.1 130.4 %reduce-scatter.38.cloned.1.call-done = f32[2,192,1536]{2,1,0:T(8,128)} async-done(((f32[2,1536,1536]{2,1,0:T(8,128)}), f32[2,192,1536]{2,1,0:T(8,128)}) %reduce-scatter.38.cloned.1.call-update) | async-done | bytes 2359312 | tf_op jit(solution)/shard_map/reduce_scatter | solution.py:464
  1400.5 103.6 %reduce-scatter.32.cloned.1.call-done = f32[2,192,3,384]{3,1,2,0:T(8,128)} async-done(((f32[2,1536,3,384]{3,1,2,0:T(8,128)}), f32[2,192,3,384]{3,1,2,0:T(8,128)}) %reduce-scatter.32.cloned.1.call-update) | async-done | bytes 1769488 | tf_op jit(solution)/shard_map/reduce_scatter | solution.py:461
  (591 shorter events, 265.6 us)
Async XLA Ops:
  8.1 19.8 %copy-start.46 = (bf16[2,64,384]{2,1,0:T(8,128)(2,1)S(1)}, bf16[2,64,384]{2,1,0:T(8,128)(2,1)}, u32[]{:S(2)}) copy-start(bf16[2,64,384]{2,1,0:T(8,128)(2,1)} %param.25) | copy-start | bytes 294916
  8.1 176.4 %all-reduce.8.cloned.1.call-start = ((), (), s32[]{:S(2)}) async-start(), calls=%async_computation.20 | async-start | bytes 589824 | tf_op jit(solution)/shard_map/psum | solution.py:200
  11.6 16.2 %copy-start.64 = (f32[4,1536]{1,0:T(4,128)}, f32[4,1536]{1,0:T(4,128)S(1)}, u32[]{:S(2)}) copy-start(f32[4,1536]{1,0:T(4,128)S(1)} %select_convert_fusion) | copy-start | bytes 73732
  13.6 173.2 %all-gather.9.cloned.1.call-start = ((), (), s32[]{:S(2)}) async-start(), calls=%async_computation.21 | async-start | bytes 1966080 | tf_op jit(solution)/shard_map/all_gather | solution.py:59
  14.2 176.4 %all-gather.11.cloned.1.call-start = ((), (), s32[]{:S(2)}) async-start(), calls=%async_computation.22 | async-start | bytes 7962624 | tf_op jit(solution)/shard_map/all_gather | solution.py:204
  14.7 271.8 %all-gather.13.cloned.1.call-start = ((), (), s32[]{:S(2)}) async-start(), calls=%async_computation.23 | async-start | bytes 2654208 | tf_op jit(solution)/shard_map/all_gather | solution.py:205
  48.3 142.2 %copy-start.19 = (bf16[2,64,1536]{2,1,0:T(8,128)(2,1)}, bf16[2,64,1536]{2,1,0:T(8,128)(2,1)S(1)}, u32[]{:S(2)}) copy-start(bf16[2,64,1536]{2,1,0:T(8,128)(2,1)S(1)} %all_gather.51) | copy-start | bytes 1179652
  48.4 142.1 %copy-start.94 = (f32[2,64]{1,0:T(2,128)}, f32[2,64]{1,0:T(2,128)S(1)}, u32[]{:S(2)}) copy-start(f32[2,64]{1,0:T(2,128)S(1)} %broadcast_multiply_fusion.11) | copy-start | bytes 1540
  48.7 141.9 %copy-start.101 = (f32[2,64]{1,0:T(2,128)}, f32[2,64]{1,0:T(2,128)S(1)}, u32[]{:S(2)}) copy-start(f32[2,64]{1,0:T(2,128)S(1)} %add_rsqrt_fusion.3) | copy-start | bytes 1540
  186.2 18.7 %copy-start.78 = (f32[2,1536]{1,0:T(2,128)}, f32[2,1536]{1,0:T(2,128)S(1)}, u32[]{:S(2)}) copy-start(f32[2,1536]{1,0:T(2,128)S(1)} %get-tuple-element.388) | copy-start | bytes 36868
  186.2 18.7 %copy-start.80 = (f32[2,1536]{1,0:T(2,128)}, f32[2,1536]{1,0:T(2,128)S(1)}, u32[]{:S(2)}) copy-start(f32[2,1536]{1,0:T(2,128)S(1)} %get-tuple-element.389) | copy-start | bytes 36868
  188.5 16.4 %copy-start.70 = (f32[2,256]{1,0:T(2,128)}, f32[2,256]{1,0:T(2,128)S(1)}, u32[]{:S(2)}) copy-start(f32[2,256]{1,0:T(2,128)S(1)} %broadcast_multiply_fusion.5) | copy-start | bytes 6148
  190.5 14.4 copy-start.96
  200.7 12.1 all-to-all-start.1
  212.8 19.3 %all-to-all-start = ((bf16[3,12,256,64]{2,3,0,1:T(8,128)(2,1)}), bf16[3,12,256,64]{2,3,0,1:T(8,128)(2,1)S(1)}, u32[]{:S(2)}, u32[]{:S(2)}) async-start(bf16[3,12,256,64]{2,3,0,1:T(8,128)(2,1)} %copy.256), calls=%async_computation | async-start | bytes 2359296 | tf_op jit(solution)/shard_map/all_to_all | solution.py:235
  216.4 135.7 %reduce-scatter.16.cloned.1.call-start = ((), (), s32[]{:S(2)}) async-start(), calls=%async_computation.24 | async-start | bytes 3932160 | tf_op jit(solution)/shard_map/reduce_scatter | solution.py:66
  264.5 20.5 %copy-start.18 = (bf16[3,1280,64]{1,2,0:T(8,128)(2,1)}, bf16[3,1280,64]{1,2,0:T(8,128)(2,1)S(1)}, u32[]{:S(2)}) copy-start(bf16[3,1280,64]{1,2,0:T(8,128)(2,1)S(1)} %get-tuple-element.596) | copy-start | bytes 1474564
  286.5 65.6 %copy-start.36 = (bf16[2,256,384]{2,1,0:T(8,128)(2,1)S(1)}, bf16[2,256,384]{2,1,0:T(8,128)(2,1)}, u32[]{:S(2)}) copy-start(bf16[2,256,384]{2,1,0:T(8,128)(2,1)} %param.24) | copy-start | bytes 1179652
  290.6 64.4 %copy-start.29 = (bf16[2,256,384]{2,1,0:T(8,128)(2,1)S(1)}, bf16[2,256,384]{2,1,0:T(8,128)(2,1)}, u32[]{:S(2)}) copy-start(bf16[2,256,384]{2,1,0:T(8,128)(2,1)} %param.40) | copy-start | bytes 1179652
  290.7 126.8 %all-gather.15.cloned.1.call-start = ((), (), s32[]{:S(2)}) async-start(), calls=%async_computation.25 | async-start | bytes 3932160 | tf_op jit(solution)/shard_map/all_gather | solution.py:275
  354.2 122.4 %all-gather.17.cloned.1.call-start = ((), (), s32[]{:S(2)}) async-start(), calls=%async_computation.26 | async-start | bytes 10616832 | tf_op jit(solution)/shard_map/all_gather | solution.py:206
  355.0 160.3 %all-gather.21.cloned.1.call-start = ((), (), s32[]{:S(2)}) async-start(), calls=%async_computation.31 | async-start | bytes 1966080 | tf_op jit(solution)/shard_map/all_gather | solution.py:59
  355.9 219.0 %all-gather.19.cloned.1.call-start = ((), (), s32[]{:S(2)}) async-start(), calls=%async_computation.27 | async-start | bytes 10616832 | tf_op jit(solution)/shard_map/all_gather | solution.py:207
  367.4 7.6 all-to-all-start.3
  370.7 250.0 %reduce-scatter.20.cloned.1.call-start = ((), (), s32[]{:S(2)}) async-start(), calls=%async_computation.29 | async-start | bytes 983040 | tf_op jit(solution)/shard_map/reduce_scatter | solution.py:67
  375.5 46.5 %copy-start.40 = (bf16[2,64,384]{2,1,0:T(8,128)(2,1)}, bf16[2,64,384]{2,1,0:T(8,128)(2,1)S(1)}, u32[]{:S(2)}) copy-start(bf16[2,64,384]{2,1,0:T(8,128)(2,1)S(1)} %reshape.337) | copy-start | bytes 294916
  378.2 98.4 %copy-start.86 = (f32[2,1536]{1,0:T(2,128)S(1)}, f32[2,1536]{1,0:T(2,128)}, u32[]{:S(2)}) copy-start(f32[2,1536]{1,0:T(2,128)} %get-tuple-element.386) | copy-start | bytes 36868
  378.3 98.4 %copy-start.88 = (f32[2,1536]{1,0:T(2,128)S(1)}, f32[2,1536]{1,0:T(2,128)}, u32[]{:S(2)}) copy-start(f32[2,1536]{1,0:T(2,128)} %get-tuple-element.387) | copy-start | bytes 36868
  378.3 306.8 %reduce-scatter.24.cloned.1.call-start = ((), (), s32[]{:S(2)}) async-start(), calls=%async_computation.32 | async-start | bytes 3932160 | tf_op jit(solution)/shard_map/reduce_scatter | solution.py:66
  419.6 170.2 %copy-start.72 = (f32[2,256]{1,0:T(2,128)}, f32[2,256]{1,0:T(2,128)S(1)}, u32[]{:S(2)}) copy-start(f32[2,256]{1,0:T(2,128)S(1)} %broadcast_multiply_fusion.4) | copy-start | bytes 6148
  422.0 167.8 %copy-start.98 = (f32[2,256]{1,0:T(2,128)}, f32[2,256]{1,0:T(2,128)S(1)}, u32[]{:S(2)}) copy-start(f32[2,256]{1,0:T(2,128)S(1)} %add_rsqrt_fusion) | copy-start | bytes 6148
  592.4 149.0 %reduce-scatter.18.cloned.1.call-start = ((), (), s32[]{:S(2)}) async-start(), calls=%async_computation.28 | async-start | bytes 3932160 | tf_op jit(solution)/shard_map/reduce_scatter | solution.py:66
  600.2 20.5 %copy-start.47 = (bf16[2,64,384]{2,1,0:T(8,128)(2,1)S(1)}, bf16[2,64,384]{2,1,0:T(8,128)(2,1)}, u32[]{:S(2)}) copy-start(bf16[2,64,384]{2,1,0:T(8,128)(2,1)} %param.25) | copy-start | bytes 294916
  600.2 20.5 %copy-start.65 = (f32[2,384]{1,0:T(2,128)S(1)}, f32[2,384]{1,0:T(2,128)}, u32[]{:S(2)}) copy-start(f32[2,384]{1,0:T(2,128)} %get-tuple-element.376) | copy-start | bytes 9220
  600.3 167.1 %reduce-scatter.26.cloned.1.call-start = ((), (), s32[]{:S(2)}) async-start(), calls=%async_computation.34 | async-start | bytes 983040 | tf_op jit(solution)/shard_map/reduce_scatter | solution.py:67
  601.1 19.6 %copy-start.69 = (f32[384]{0:T(512)}, f32[384]{0:T(512)S(1)}, u32[]{:S(2)}) copy-start(f32[384]{0:T(512)S(1)} %add.444) | copy-start | bytes 4612
  651.8 12.7 copy-start.11
  653.3 11.2 copy-start.67
  653.6 11.0 copy-start.74
  665.8 75.6 %copy-start.17 = (f32[2,256,384]{2,1,0:T(8,128)S(1)}, f32[2,256,384]{2,1,0:T(8,128)}, u32[]{:S(2)}) copy-start(f32[2,256,384]{2,1,0:T(8,128)} %multiply_add_fusion.2) | copy-start | bytes 2359300
  665.8 126.5 %reduce-scatter.22.cloned.1.call-start = ((), (), s32[]{:S(2)}) async-start(), calls=%async_computation.30 | async-start | bytes 983040 | tf_op jit(solution)/shard_map/reduce_scatter | solution.py:67
  671.1 161.8 %all-gather.23.cloned.1.call-start = ((), (), s32[]{:S(2)}) async-start(), calls=%async_computation.33 | async-start | bytes 1966080 | tf_op jit(solution)/shard_map/all_gather | solution.py:59
  816.2 7.6 all-to-all-start.5
  824.1 16.1 %copy-start.77 = (f32[2,384]{1,0:T(2,128)S(1)}, f32[2,384]{1,0:T(2,128)}, u32[]{:S(2)}) copy-start(f32[2,384]{1,0:T(2,128)} %get-tuple-element.302) | copy-start | bytes 9220
  824.1 16.7 %copy-start.76 = (f32[2,384]{1,0:T(2,128)S(1)}, f32[2,384]{1,0:T(2,128)}, u32[]{:S(2)}) copy-start(f32[2,384]{1,0:T(2,128)} %get-tuple-element.308) | copy-start | bytes 9220
  836.6 11.0 all-to-all-start.4
  945.1 12.2 all-to-all-start.7
  957.3 12.5 copy-start.20
  957.3 12.5 copy-start.54
  957.3 12.5 copy-start.95
  958.1 19.3 %all-to-all-start.6 = ((bf16[4,2,73728]{2,1,0:T(2,128)(2,1)}), bf16[4,2,73728]{2,1,0:T(2,128)(2,1)S(1)}, u32[]{:S(2)}, u32[]{:S(2)}) async-start(bf16[4,2,73728]{2,1,0:T(2,128)(2,1)} %reshape.438), calls=%async_computation.12 | async-start | bytes 2359296 | tf_op jit(solution)/shard_map/all_to_all | solution.py:381
  961.6 202.6 %all-reduce.10.cloned.1.call-start = ((), (), s32[]{:S(2)}) async-start(), calls=%async_computation.37 | async-start | bytes 589824 | tf_op jit(solution)/shard_map/psum | solution.py:438
  994.5 181.8 %reduce-scatter.30.cloned.1.call-start = ((), (), s32[]{:S(2)}) async-start(), calls=%async_computation.36 | async-start | bytes 983040 | tf_op jit(solution)/shard_map/reduce_scatter | solution.py:67
  997.0 180.9 %reduce-scatter.28.cloned.1.call-start = ((), (), s32[]{:S(2)}) async-start(), calls=%async_computation.35 | async-start | bytes 3932160 | tf_op jit(solution)/shard_map/reduce_scatter | solution.py:66
  1001.7 178.4 %reduce-scatter.34.cloned.1.call-start = ((), (), s32[]{:S(2)}) async-start(), calls=%async_computation.39 | async-start | bytes 5308416 | tf_op jit(solution)/shard_map/reduce_scatter | solution.py:462
  1008.6 261.5 %reduce-scatter.36.cloned.1.call-start = ((), (), s32[]{:S(2)}) async-start(), calls=%async_computation.40 | async-start | bytes 21233664 | tf_op jit(solution)/shard_map/reduce_scatter | solution.py:463
  1021.8 378.6 %reduce-scatter.38.cloned.1.call-start = ((), (), s32[]{:S(2)}) async-start(), calls=%async_computation.41 | async-start | bytes 21233664 | tf_op jit(solution)/shard_map/reduce_scatter | solution.py:464
  1034.5 469.6 %reduce-scatter.32.cloned.1.call-start = ((), (), s32[]{:S(2)}) async-start(), calls=%async_computation.38 | async-start | bytes 15925248 | tf_op jit(solution)/shard_map/reduce_scatter | solution.py:461
  1056.2 11.6 copy-start.22
  1056.2 11.7 copy-start.25
  1094.7 81.6 %copy-start.43 = (bf16[2,64,384]{2,1,0:T(8,128)(2,1)S(1)}, bf16[2,64,384]{2,1,0:T(8,128)(2,1)}, u32[]{:S(2)}) copy-start(bf16[2,64,384]{2,1,0:T(8,128)(2,1)} %param.41) | copy-start | bytes 294916
  1094.7 81.6 %copy-start.44 = (f32[2,64,384]{2,1,0:T(8,128)S(1)}, f32[2,64,384]{2,1,0:T(8,128)}, u32[]{:S(2)}) copy-start(f32[2,64,384]{2,1,0:T(8,128)} %reduce-scatter.26.cloned.1.call-done) | copy-start | bytes 589828
  1094.7 83.3 %copy-start.30 = (bf16[2,256,384]{2,1,0:T(8,128)(2,1)S(1)}, bf16[2,256,384]{2,1,0:T(8,128)(2,1)}, u32[]{:S(2)}) copy-start(bf16[2,256,384]{2,1,0:T(8,128)(2,1)} %param.40) | copy-start | bytes 1179652
  1094.7 83.3 %copy-start.33 = (f32[2,256,384]{2,1,0:T(8,128)S(1)}, f32[2,256,384]{2,1,0:T(8,128)}, u32[]{:S(2)}) copy-start(f32[2,256,384]{2,1,0:T(8,128)} %reduce-scatter.24.cloned.1.call-done) | copy-start | bytes 2359300
  (91 other events, 375.8 us)
Sparse Core Ops, SparseCore 0:
  14.8 169.6 all-reduce.7
  994.6 169.6 all-reduce.9
Sparse Core Ops, SparseCore 1:
  15.6 46.6 all-gather.8
  64.0 47.9 all-gather.10
  113.8 28.7 all-gather.12
  290.7 61.3 reduce-scatter.15
  354.3 63.1 all-gather.14
  419.4 57.2 all-gather.16
  478.7 36.5 all-gather.20
  517.0 57.8 all-gather.18
  577.6 23.2 reduce-scatter.19
  603.8 75.6 reduce-scatter.23
  681.7 59.7 reduce-scatter.17
  744.3 23.1 reduce-scatter.25
  769.6 22.6 reduce-scatter.21
  794.4 38.4 all-gather.22
  998.2 21.7 reduce-scatter.29
  1022.2 59.8 reduce-scatter.27
  1086.0 53.4 reduce-scatter.33
  1143.8 126.3 reduce-scatter.35
  1274.2 126.2 reduce-scatter.37
  1404.6 99.4 reduce-scatter.31
where the time goes:
time: 1520 us; the launch traced here: 1510 us
  waiting for transfers between devices  903 us (59%)
  matrix products  190 us (12%)
  blocking collectives  159 us (10%)
  local copies, waits for them, and re-layouts  129 us (8%)
  other arithmetic  84.3 us (6%)
  starting transfers between devices  27.3 us (2%)
  between operations  18.1 us (1%)
    psum x1, waiting for transfers between devices, body(): mod_all = lax.psum(mod_term + bias_wide[None], ('shard', 'ctx', 'tp'))  136 us
    reduce_scatter x1, waiting for transfers between devices, body(): lax.psum_scatter(grad_terms[3], ('shard', 'ctx'), scatter_dimension=1, ti...  130 us
    reduce_scatter x4, waiting for transfers between devices, part_sums(): lax.psum_scatter(arrays[0], 'tp', scatter_dimension=2, tiled=True)  105 us
    reduce_scatter x1, waiting for transfers between devices, body(): lax.psum_scatter(grad_terms[0], ('shard', 'ctx'), scatter_dimension=1, ti...  104 us
    reduce_scatter x1, waiting for transfers between devices, body(): lax.psum_scatter(grad_terms[2], ('shard', 'ctx'), scatter_dimension=1, ti...  90 us
    psum x1, waiting for transfers between devices, body(): grad_mod = lax.psum(mod_place, ('shard', 'ctx', 'tp'))  69.6 us
    all_gather x1, waiting for transfers between devices, body(): lax.all_gather(fc2_weight, ('shard', 'ctx'), axis=1, tiled=True)  59.6 us
    all_gather x3, blocking collectives, full_width(): lax.all_gather(arrays[1], 'tp', axis=2, tiled=True)  57 us
  transfers between devices with their start and end apart: 29, of which 19 were waited for; matrix products, arithmetic and copies ran while one was open for 17% of the time, Pallas kernels for 0%

commit v1 on v0

v1 whole, which is shorter than its diff:
```python
from functools import partial
import math

import jax
import jax.numpy as jnp
from jax import lax
from jax.experimental import pallas as pl
from jax.experimental.pallas import tpu as pltpu
from jax.sharding import PartitionSpec as P

HD = 64
PAIR = 2 * HD
LI = 1024
LT = 256
SCALE = 1.0 / math.sqrt(HD)

EPSILON = 1e-06
NEG_LARGE = -1e30
GELU_COEF = math.sqrt(2.0 / math.pi)
PRECISE = lax.Precision.HIGHEST
BF = jnp.bfloat16
F32 = jnp.float32

NT = (((1,), (1,)), ((), ()))
TN = (((0,), (0,)), ((), ()))


def layer_norm(values):
    mean = jnp.mean(values, -1, keepdims=True)
    center = values - mean
    inv_std = lax.rsqrt(jnp.mean(center * center, -1, keepdims=True) + EPSILON)
    return (center * inv_std, inv_std, mean)


def norm_back(normed, inv_std, grad_in):
    return inv_std * (
        grad_in
        - jnp.mean(grad_in, -1, keepdims=True)
        - normed * jnp.mean(grad_in * normed, -1, keepdims=True)
    )


def gelu_tanh(values):
    return (
        0.5 * values * (1.0 + jnp.tanh(GELU_COEF * (values + 0.044715 * values * values * values)))
    )


def gelu_slope(values):
    tanh_val = jnp.tanh(GELU_COEF * (values + 0.044715 * values * values * values))
    return 0.5 * (1.0 + tanh_val) + 0.5 * values * (1.0 - tanh_val * tanh_val) * GELU_COEF * (
        1.0 + 0.134145 * values * values
    )


def silu_slope(values):
    sigmoid = jax.nn.sigmoid(values)
    return sigmoid * (1.0 + values * (1.0 - sigmoid))


def after(value, *deps):
    return lax.optimization_barrier((value,) + deps)[0]


def attend_kernel(count, q_ref, bias_ref, *refs):
    kv_refs, (o_ref, l_ref) = refs[:count], refs[count:]
    keys = jnp.concatenate([r[0] for r in kv_refs], 0)
    vals = jnp.concatenate([r[1] for r in kv_refs], 0)
    bias = bias_ref[0]
    outs, logs = [], []
    for half in range(2):
        cols = slice(half * HD, (half + 1) * HD)
        query = q_ref[:, cols] * SCALE
        scores = lax.dot_general(query, keys[:, cols], NT, preferred_element_type=F32) + bias
        top = jnp.max(scores, 1, keepdims=True)
        weights = jnp.exp(scores - top)
        total = jnp.sum(weights, 1, keepdims=True)
        mixed = jnp.dot(weights.astype(BF), vals[:, cols], preferred_element_type=F32)
        outs.append((mixed / total).astype(BF))
        logs.append(jnp.broadcast_to(top + jnp.log(total), (query.shape[0], HD)))
    o_ref[...] = jnp.concatenate(outs, 1)
    l_ref[...] = jnp.concatenate(logs, 1)


def attend_back_kernel(count, q_ref, bias_ref, o_ref, g_ref, l_ref, *refs):
    kv_refs, dq_ref, out_refs = refs[:count], refs[count], refs[count + 1 :]
    keys = jnp.concatenate([r[0] for r in kv_refs], 0)
    vals = jnp.concatenate([r[1] for r in kv_refs], 0)
    bias = bias_ref[0]
    grads_q, grads_k, grads_v = [], [], []
    for half in range(2):
        cols = slice(half * HD, (half + 1) * HD)
        query = q_ref[:, cols] * SCALE
        grad = g_ref[:, cols]
        delta = jnp.sum(grad.astype(F32) * o_ref[:, cols].astype(F32), 1, keepdims=True)
        log_total = l_ref[:, half * HD : half * HD + 1]
        scores = lax.dot_general(query, keys[:, cols], NT, preferred_element_type=F32) + bias
        probs = jnp.exp(scores - log_total)
        grad_prob = lax.dot_general(grad, vals[:, cols], NT, preferred_element_type=F32)
        grad_scores = (probs * (grad_prob - delta)).astype(BF)
        grads_q.append(
            (jnp.dot(grad_scores, keys[:, cols], preferred_element_type=F32) * SCALE).astype(BF)
        )
        grads_k.append(lax.dot_general(grad_scores, query, TN, preferred_element_type=F32))
        grads_v.append(
            lax.dot_general(probs.astype(BF), grad, TN, preferred_element_type=F32)
        )
    dq_ref[...] = jnp.concatenate(grads_q, 1)
    grad_k = jnp.concatenate(grads_k, 1).astype(BF)
    grad_v = jnp.concatenate(grads_v, 1).astype(BF)
    rows = q_ref.shape[0]
    for at in range(count):
        out_refs[at][0] = grad_k[at * rows : (at + 1) * rows]
        out_refs[at][1] = grad_v[at * rows : (at + 1) * rows]


def attention_specs(slots, rows, count):
    row_spec = pl.BlockSpec((rows, PAIR), lambda s, h: (s, h))
    bias_spec = pl.BlockSpec((1, 1, count * rows), lambda s, h: (s, 0, 0))
    kv_spec = pl.BlockSpec((2, rows, PAIR), lambda s, h: (0, s, h))
    return row_spec, bias_spec, kv_spec


def attend(query, bias, pieces):
    slots, count = bias.shape[0], len(pieces)
    rows = query.shape[0] // slots
    row_spec, bias_spec, kv_spec = attention_specs(slots, rows, count)
    return pl.pallas_call(
        partial(attend_kernel, count),
        grid=(slots, query.shape[1] // PAIR),
        in_specs=[row_spec, bias_spec] + [kv_spec] * count,
        out_specs=[row_spec, row_spec],
        out_shape=[
            jax.ShapeDtypeStruct(query.shape, BF),
            jax.ShapeDtypeStruct(query.shape, F32),
        ],
        name="attend",
    )(query, bias, *pieces)


def attend_back(query, bias, mixed, grad, log_total, pieces):
    slots, count = bias.shape[0], len(pieces)
    rows = query.shape[0] // slots
    row_spec, bias_spec, kv_spec = attention_specs(slots, rows, count)
    return pl.pallas_call(
        partial(attend_back_kernel, count),
        grid=(slots, query.shape[1] // PAIR),
        in_specs=[row_spec, bias_spec, row_spec, row_spec, row_spec] + [kv_spec] * count,
        out_specs=[row_spec] + [kv_spec] * count,
        out_shape=[jax.ShapeDtypeStruct(query.shape, BF)]
        + [jax.ShapeDtypeStruct(pieces[0].shape, BF)] * count,
        name="attend_back",
    )(query, bias, mixed, grad, log_total, *pieces)


def body(
    sizes,
    image_tokens,
    text_tokens,
    conditioning,
    seq_table,
    image_len,
    text_len,
    mod_weight,
    mod_bias,
    qkv_weight,
    qkv_bias,
    out_weight,
    out_bias,
    fc1_weight,
    fc1_bias,
    fc2_weight,
    fc2_bias,
    image_cot,
    text_cot,
):
    n_shard, n_ctx, n_tp = sizes
    group = image_tokens.shape[0]
    n_img, n_txt = image_tokens.shape[1], text_tokens.shape[1]
    rows = n_img + n_txt
    cols = image_tokens.shape[2]
    heads = cols // HD
    width = conditioning.shape[1]
    hidden_cols = fc1_weight.shape[2]
    owned_rows = mod_weight.shape[1]
    my_shard, my_ctx, my_tp = (
        lax.axis_index("shard"),
        lax.axis_index("ctx"),
        lax.axis_index("tp"),
    )
    row_begin = lax.axis_index(("shard", "ctx", "tp")) * owned_rows
    owner = lax.axis_index(("shard", "ctx"))
    n_owner = n_shard * n_ctx
    first_slot = my_shard * group

    def rotate(value, axis, size, step):
        return lax.ppermute(value, axis, [(i, (i + step) % size) for i in range(size)])

    def flip(value, bit):
        return lax.ppermute(value, "ctx", [(i, i ^ bit) for i in range(n_ctx)])

    def own_cols(value):
        return lax.dynamic_slice_in_dim(value, my_tp * cols, cols, value.ndim - 1)

    def pack(parts):
        return jnp.concatenate(parts, 1)

    def split(value):
        return (value[:, :n_img], value[:, n_img:])

    def gather_tp(value):
        wide = jnp.zeros(value.shape[:-1] + (width,), value.dtype)
        lead = (0,) * (value.ndim - 1)
        wide = lax.dynamic_update_slice(wide, value, lead + (my_tp * cols,))
        for step in (2, 1, 3):
            piece = rotate(value, "tp", n_tp, step)
            source = lax.rem(my_tp + n_tp - step, n_tp)
            wide = lax.dynamic_update_slice(wide, piece, lead + (source * cols,))
        return wide

    def scatter_tp(parts):
        packed = pack([p.astype(BF) for p in parts])
        total = own_cols(packed).astype(F32)
        for step in (2, 1, 3):
            target = lax.rem(my_tp + step, n_tp)
            piece = lax.dynamic_slice_in_dim(packed, target * cols, cols, 2)
            total = total + rotate(piece, "tp", n_tp, step).astype(F32)
        return total

    def sum_ctx(value):
        value = value + flip(value, 1)
        return value + flip(value, 2)

    def sum_tp(value):
        total = value
        for step in range(1, n_tp):
            total = total + rotate(value, "tp", n_tp, step)
        return total

    flat_qkv = qkv_weight.reshape(2, qkv_weight.shape[1], 3 * cols)
    w_qkv, w_out, w_fc1, w_fc2 = (
        lax.all_gather(w, ("shard", "ctx"), axis=1, tiled=True)
        for w in (flat_qkv, out_weight, fc1_weight, fc2_weight)
    )

    tokens = pack([image_tokens, text_tokens])
    wide_in = gather_tp(tokens)

    cond_rows = jnp.take(conditioning, seq_table, axis=0).astype(F32)
    cond_act = jax.nn.silu(cond_rows)
    act_part = lax.dynamic_slice_in_dim(cond_act, row_begin, owned_rows, 1)
    mod_local = mod_weight.astype(F32)
    mod_term = jnp.einsum("sr,xrke->sxke", act_part, mod_local, precision=PRECISE)
    bias_wide = lax.dynamic_update_slice(
        jnp.zeros(mod_bias.shape[:2] + (width,), F32), mod_bias.astype(F32), (0, 0, row_begin)
    )
    mod_term = (mod_term + bias_wide[None]).reshape(n_shard, group * 12, width)
    bias_flat = jnp.concatenate(
        [b.reshape(-1) for b in (qkv_bias, out_bias, fc1_bias, fc2_bias)]
    ).astype(F32)
    bias_rows = lax.dynamic_update_slice(
        jnp.zeros((n_owner, bias_flat.shape[0]), F32), bias_flat[None], (owner, 0)
    ).reshape(-1, width)

    def mod_message(which):
        return jnp.concatenate(
            [lax.dynamic_index_in_dim(mod_term, which, 0, keepdims=False), bias_rows], 0
        )

    message = mod_message(my_shard)
    for step in range(1, n_shard):
        message = message + rotate(
            mod_message(lax.rem(my_shard + step, n_shard)), "shard", n_shard, step
        )
    message = sum_ctx(message)
    mod_here = sum_tp(message[: group * 12]).reshape(group, 2, 6, width)
    gate_cols = own_cols(mod_here)
    bias_all = message[group * 12 :].reshape(n_owner, -1)
    bias_parts, begin = [], 0
    for b in (qkv_bias, out_bias, fc1_bias, fc2_bias):
        part = bias_all[:, begin : begin + b.size].reshape((n_owner,) + b.shape)
        begin += b.size
        part = jnp.moveaxis(part, 0, -2)
        bias_parts.append(part.reshape(b.shape[:-1] + (HD,)))
    b_qkv = bias_parts[0].reshape(2, 2, cols)
    bias_three = jnp.concatenate([b_qkv[:, 0], jnp.zeros((2, cols), F32), b_qkv[:, 1]], 1)
    b_out = bias_parts[1].reshape(2, cols)
    b_fc1 = bias_parts[2].reshape(2, hidden_cols)
    b_fc2 = bias_parts[3].reshape(2, cols)

    piece_ctx = [my_ctx, my_ctx ^ 1, my_ctx ^ 2, my_ctx ^ 3]
    here = lambda a: lax.dynamic_slice_in_dim(a, first_slot, group, 0)[:, None]
    image_here, text_here = here(image_len), here(text_len)
    valid = []
    for at in piece_ctx:
        valid.append(at * n_img + jnp.arange(n_img)[None] < image_here)
        valid.append(at * n_txt + jnp.arange(n_txt)[None] < text_here)
    key_bias = jnp.where(jnp.concatenate(valid, 1), 0.0, NEG_LARGE).astype(F32)[:, None]

    cot_wide = gather_tp(after(pack([image_cot, text_cot]), wide_in))

    def mods(which):
        return lambda stream: mod_here[:, stream, which, None]

    shift1, scale1, _, shift2, scale2, _ = (mods(j) for j in range(6))
    gates1 = [gate_cols[:, s, 2, None] for s in range(2)]
    gates2 = [gate_cols[:, s, 5, None] for s in range(2)]

    def dot(spec, a, b):
        return jnp.einsum(spec, a, b, preferred_element_type=F32)

    normed_one, inv_one, mean_one, hidden_one, packed = ([], [], [], [], [])
    for stream, values in enumerate(split(wide_in)):
        normed, inv_std, mean = layer_norm(values.astype(F32))
        hidden = (normed * (1.0 + scale1(stream)) + shift1(stream)).astype(BF)
        normed_one.append(normed)
        inv_one.append(inv_std)
        mean_one.append(mean)
        hidden_one.append(hidden)
        packed.append((dot("snd,dh->snh", hidden, w_qkv[stream]) + bias_three[stream]).astype(BF))
    packed = pack(packed).reshape(group * rows, 3 * cols)
    query = packed[:, :cols]
    kv_own = jnp.stack([packed[:, cols : 2 * cols], packed[:, 2 * cols :]], 0)
    kv_x = flip(kv_own, 2)
    kv_core = flip(kv_own, 1)
    kv_xcore = flip(kv_x, 1)
    pieces = (kv_own, kv_core, kv_x, kv_xcore)
    mixed, log_total = attend(query, key_bias, pieces)
    mixed_tok = split(mixed.reshape(group, rows, cols))
    attn = scatter_tp([dot("snh,oh->sno", mixed_tok[s], w_out[s]) for s in range(2)])
    branch_one, resid, sent = ([], [], [])
    inputs = (image_tokens, text_tokens)
    for stream, values in enumerate(split(attn)):
        branch = values + b_out[stream]
        branch_one.append(branch)
        resid.append(inputs[stream].astype(F32) + gates1[stream] * branch)
        sent.append((resid[stream] - mean_one[stream]).astype(BF))
    wide_resid = gather_tp(pack(sent))

    normed_two, inv_two, hidden_two, pre_act, act_two = ([], [], [], [], [])
    for stream, values in enumerate(split(wide_resid)):
        normed, inv_std, _ = layer_norm(values.astype(F32))
        hidden = (normed * (1.0 + scale2(stream)) + shift2(stream)).astype(BF)
        pre_values = dot("snd,df->snf", hidden, w_fc1[stream]) + b_fc1[stream]
        normed_two.append(normed)
        inv_two.append(inv_std)
        hidden_two.append(hidden)
        pre_act.append(pre_values)
        act_two.append(gelu_tanh(pre_values).astype(BF))
    grad_two_wide = [
        (c.astype(F32) * mod_here[:, s, 5, None]).astype(BF) for s, c in enumerate(split(cot_wide))
    ]
    fc1_bias_sums, grad_act_half, grad_hidden_two, back_two = ([], [], [], [])
    for stream in range(2):
        grad_act = dot("sno,of->snf", grad_two_wide[stream], w_fc2[stream]) * gelu_slope(
            pre_act[stream]
        )
        fc1_bias_sums.append(jnp.sum(grad_act, (0, 1)))
        grad_act_half.append(grad_act.astype(BF))
        grad_hidden = dot("snf,df->snd", grad_act_half[stream], w_fc1[stream])
        grad_hidden_two.append(grad_hidden)
        back_two.append(
            norm_back(
                normed_two[stream], inv_two[stream], grad_hidden * (1.0 + scale2(stream))
            )
        )
    back_two_sum = split(scatter_tp(back_two))
    fc2_grads = [dot("sno,snf->of", grad_two_wide[s], act_two[s]).astype(BF) for s in range(2)]
    fc1_grads = [dot("snd,snf->df", hidden_two[s], grad_act_half[s]).astype(BF) for s in range(2)]
    cots = [c.astype(F32) for c in (image_cot, text_cot)]
    grad_resid = [cots[s] + back_two_sum[s] for s in range(2)]
    grad_one = [grad_resid[s] * gates1[s] for s in range(2)]
    grad_one_wide = gather_tp(pack([g.astype(BF) for g in grad_one]))

    out_grads, grad_mixed = ([], [])
    for stream, values in enumerate(split(grad_one_wide)):
        grad_mixed.append(dot("sno,oh->snh", values, w_out[stream]).astype(BF))
        out_grads.append(dot("sno,snh->oh", values, mixed_tok[stream]).astype(BF))
    grad_mixed = pack(grad_mixed).reshape(group * rows, cols)
    grad_query, *grad_kv = attend_back(query, key_bias, mixed, grad_mixed, log_total, pieces)
    grad_own, grad_core, grad_x, grad_xcore = grad_kv
    from_core = flip(jnp.stack([grad_core, grad_xcore], 0), 1)
    sum_x = (grad_x.astype(F32) + from_core[1].astype(F32)).astype(BF)
    from_x = flip(sum_x, 2)
    grad_key_value = (
        grad_own.astype(F32) + from_core[0].astype(F32) + from_x.astype(F32)
    ).astype(BF)

    mlp_parts = [dot("snf,of->sno", act_two[s], w_fc2[s]) for s in range(2)]
    mlp_sum = split(scatter_tp(after(tuple(mlp_parts), grad_one_wide)))
    branch_two = [mlp_sum[s] + b_fc2[s] for s in range(2)]
    outputs = [(resid[s] + gates2[s] * branch_two[s]).astype(BF) for s in range(2)]

    grad_packed = jnp.concatenate([grad_query, grad_key_value[0], grad_key_value[1]], 1)
    grad_tok = split(grad_packed.reshape(group, rows, 3 * cols))
    qkv_grads, qkv_bias_sums, grad_hidden_one, back_one = ([], [], [], [])
    for stream in range(2):
        qkv_grads.append(dot("snd,snh->dh", hidden_one[stream], grad_tok[stream]).astype(BF))
        bias_sum = jnp.sum(grad_tok[stream], (0, 1), dtype=F32)
        qkv_bias_sums.append(jnp.concatenate([bias_sum[:cols], bias_sum[2 * cols :]]))
        grad_hidden = dot("snh,dh->snd", grad_tok[stream], w_qkv[stream])
        grad_hidden_one.append(grad_hidden)
        back_one.append(
            norm_back(
                normed_one[stream], inv_one[stream], grad_hidden * (1.0 + scale1(stream))
            )
        )
    back_one_sum = split(scatter_tp(back_one))
    input_grads = [grad_resid[s] + back_one_sum[s] for s in range(2)]

    def place_cols(values):
        return lax.dynamic_update_slice(
            jnp.zeros((group, width), F32), values, (0, my_tp * cols)
        )

    def all_slots(pieces_of, extra):
        mod_rows = jnp.stack([jnp.stack(p, 1) for p in pieces_of], 1)
        count = mod_rows.shape[2]
        mod_rows = mod_rows.reshape(-1, width)
        lead = mod_rows.shape[0]
        both = sum_ctx(jnp.concatenate([mod_rows, extra.reshape(-1, width)], 0))
        both = jnp.concatenate([sum_tp(both[:lead]), both[lead:]], 0)
        slots = jnp.zeros((n_shard, lead, width), F32)
        slots = lax.dynamic_update_slice(slots, both[None, :lead], (my_shard, 0, 0))
        sums = both[lead:]
        for step in range(1, n_shard):
            other = rotate(both, "shard", n_shard, step)
            source = lax.rem(my_shard + n_shard - step, n_shard)
            slots = lax.dynamic_update_slice(slots, other[None, :lead], (source, 0, 0))
            sums = sums + other[lead:]
        return slots.reshape(n_shard * group, 2, count, width), sums

    grad_one_sums = jnp.concatenate([jnp.sum(g, (0, 1)) for g in grad_one])
    grad_two_sums = jnp.concatenate(
        [jnp.sum(cots[s] * gates2[s], (0, 1)) for s in range(2)]
    )
    pad = jnp.zeros((-2 * (grad_one_sums.size + hidden_cols)) % width, F32)
    early = jnp.concatenate([grad_one_sums, grad_two_sums] + fc1_bias_sums + [pad])
    late_mods, early_sums = all_slots(
        [
            [
                place_cols(jnp.sum(grad_resid[s] * branch_one[s], 1)),
                jnp.sum(grad_hidden_two[s], 1),
                jnp.sum(grad_hidden_two[s] * normed_two[s], 1),
                place_cols(jnp.sum(cots[s] * branch_two[s], 1)),
            ]
            for s in range(2)
        ],
        early,
    )
    late = jnp.concatenate(qkv_bias_sums)
    late = jnp.concatenate([late, jnp.zeros((-late.size) % width, F32)])
    first_mods, late_sums = all_slots(
        [
            [jnp.sum(grad_hidden_one[s], 1), jnp.sum(grad_hidden_one[s] * normed_one[s], 1)]
            for s in range(2)
        ],
        late,
    )
    grad_mod = jnp.concatenate([first_mods, late_mods], 2)
    mod_weight_grad = jnp.einsum("sr,sxke->xrke", act_part, grad_mod, precision=PRECISE)
    mod_bias_grad = lax.dynamic_slice_in_dim(jnp.sum(grad_mod, 0), row_begin, owned_rows, 2)
    act_grad = jnp.einsum("sxke,xrke->sr", grad_mod, mod_local, precision=PRECISE)
    slot_grad = act_grad * silu_slope(
        lax.dynamic_slice_in_dim(cond_rows, row_begin, owned_rows, 1)
    )
    cond_grad = jnp.zeros((conditioning.shape[0], owned_rows), F32).at[seq_table].add(slot_grad)

    def own_bias(flat, like):
        full = flat.reshape(like.shape[:-1] + (HD,))
        return lax.dynamic_slice_in_dim(
            full, owner * like.shape[-1], like.shape[-1], like.ndim - 1
        )

    early_sums = early_sums.reshape(-1)
    half = 2 * cols
    qkv_bias_grad = own_bias(late_sums.reshape(-1)[: 2 * half], qkv_bias)
    out_bias_grad = own_bias(early_sums[:half], out_bias)
    fc2_bias_grad = own_bias(early_sums[half : 2 * half], fc2_bias)
    fc1_bias_grad = own_bias(early_sums[2 * half : 2 * half + 2 * hidden_cols], fc1_bias)

    def owned(grads):
        total = lax.psum_scatter(
            jnp.stack(grads, 0), ("shard", "ctx"), scatter_dimension=1, tiled=True
        )
        return total.astype(F32)

    fc2_weight_grad = owned(fc2_grads)
    fc1_weight_grad = owned(fc1_grads)
    out_weight_grad = owned(out_grads)
    qkv_weight_grad = owned(qkv_grads).reshape(qkv_weight.shape)
    return (
        outputs[0],
        outputs[1],
        input_grads[0],
        input_grads[1],
        cond_grad,
        mod_weight_grad,
        mod_bias_grad,
        qkv_weight_grad,
        qkv_bias_grad,
        out_weight_grad,
        out_bias_grad,
        fc1_weight_grad,
        fc1_bias_grad,
        fc2_weight_grad,
        fc2_bias_grad,
    )


def solution(mesh):
    sizes = (mesh.shape["shard"], mesh.shape["ctx"], mesh.shape["tp"])
    token = P("shard", "ctx", "tp")
    everywhere = ("shard", "ctx", "tp")
    spread = ("shard", "ctx")
    mod_w, mod_b = P(None, everywhere, None, None), P(None, None, everywhere)
    qkv_w, qkv_b = P(None, spread, None, "tp"), P(None, None, "tp", spread)
    mat, vec = P(None, spread, "tp"), P(None, "tp", spread)
    return jax.shard_map(
        partial(body, sizes),
        mesh=mesh,
        in_specs=(token, token, P(), P(), P(), P(), mod_w, mod_b, qkv_w, qkv_b)
        + (mat, vec, mat, vec, mat, vec, token, token),
        out_specs=(token, token, token, token, P(None, everywhere), mod_w, mod_b, qkv_w, qkv_b)
        + (mat, vec, mat, vec, mat, vec),
        check_vma=False,
    )
```

time: 1520 us -> 691 us (0.45)
  waiting for transfers between devices: 903 us -> 261 us
  blocking collectives: 159 us -> 0 us
  matrix products: 190 us -> 93 us
  starting transfers between devices: 27.3 us -> 111 us
  local copies, waits for them, and re-layouts: 129 us -> 91.3 us
  Pallas kernels: 0 us -> 34 us
    reduce_scatter x12 -> x4, waiting for transfers between devices: 475 us -> 22.9 us  [owned(): lax.psum_scatter(jnp.stack(grads, 0), ('shard', 'ctx'), scatter_dimension...]
    ppermute x0 -> x47, waiting for transfers between devices: none -> 237 us  [the longest x36 212 us: rotate(): lax.ppermute(value, axis, [(i, (i + step) % size) for i in range(size)])]
    psum x2 -> x0, waiting for transfers between devices: 205 us -> none  [the longest x1 136 us: body(): mod_all = lax.psum(mod_term + bias_wide[None], ('shard', 'ctx', 'tp'))]
    all_gather x8 -> x4, waiting for transfers between devices: 193 us -> 0.04 us  [body(): lax.all_gather(w, ('shard', 'ctx'), axis=1, tiled=True)]
    all_gather x8 -> x0, blocking collectives: 124 us -> none  [the longest x3 57 us: full_width(): lax.all_gather(arrays[1], 'tp', axis=2, tiled=True)]
    ppermute x0 -> x47, starting transfers between devices: none -> 110 us  [the longest x36 102 us: rotate(): lax.ppermute(value, axis, [(i, (i + step) % size) for i in range(size)])]
    dot_general x66 -> x24, matrix products: 180 us -> 83.9 us  [dot(): return jnp.einsum(spec, a, b, preferred_element_type=F32)]
    pallas_call x0 -> x2, Pallas kernels: none -> 34 us  [the longest x1 20.5 us: attend_back(): pl.pallas_call(partial(attend_back_kernel, count), grid=(slots, query.sha...]
  transfers between devices with their start and end apart: 29 -> 55, of which waited for: 19 -> 24; matrix products, arithmetic and copies ran while one was open for 17% -> 32% of each run, Pallas kernels for 0% -> 5%
where the time goes in v1:
time: 691 us; the launch traced here: 681 us
  waiting for transfers between devices  261 us (38%)
  starting transfers between devices  111 us (16%)
  matrix products  93 us (13%)
  local copies, waits for them, and re-layouts  91.3 us (13%)
  other arithmetic  74.2 us (11%)
  Pallas kernels  34 us (5%)
  between operations  17 us (2%)
    ppermute x36, waiting for transfers between devices, rotate(): lax.ppermute(value, axis, [(i, (i + step) % size) for i in range(size)])  212 us
    ppermute x36, starting transfers between devices, rotate(): lax.ppermute(value, axis, [(i, (i + step) % size) for i in range(size)])  102 us
    dot_general x24, matrix products, dot(): return jnp.einsum(spec, a, b, preferred_element_type=F32)  83.9 us
    ppermute x11, waiting for transfers between devices, flip(): return lax.ppermute(value, 'ctx', [(i, i ^ bit) for i in range(n_ctx)])  24.7 us
    unnamed x282, local copies, waits for them, and re-layouts  23 us
    reduce_scatter x4, waiting for transfers between devices, owned(): lax.psum_scatter(jnp.stack(grads, 0), ('shard', 'ctx'), scatter_dimension...  22.9 us
    another operation x4, other arithmetic, owned(): jnp.stack(grads, 0)  22.2 us
    pallas_call x1, Pallas kernels, attend_back(): pl.pallas_call(partial(attend_back_kernel, count), grid=(slots, query.sha...  20.5 us
  transfers between devices with their start and end apart: 55, of which 24 were waited for; matrix products, arithmetic and copies ran while one was open for 32% of the time, Pallas kernels for 5%

profile of v1, /device:TPU:0, one launch (start us, length us, event | category | flops | bytes accessed | tf_op | source)
XLA Modules:
  0.0 681.2 jit_solution(4238107885877601896)
XLA Ops:
  7.3 2.3 copy.221
  11.3 4.1 collective-permute-start.6
  17.0 2.2 collective-permute-start.8
  25.1 8.6 %collective-permute-done = f32[28,1536]{1,0:T(8,128)S(1)} collective-permute-done((f32[28,1536]{1,0:T(8,128)S(1)}, f32[28,1536]{1,0:T(8,128)S(1)}, u32[]{:S(2)}, u32[]{:S(2)}) %collective-permute-start) | collective-permute-done | bytes 172064 | tf_op jit(solution)/shard_map/ppermute | solution.py:197
  36.8 11.9 %collective-permute-done.6 = bf16[2,320,384]{2,1,0:T(8,128)(2,1)} collective-permute-done((bf16[2,320,384]{2,1,0:T(8,128)(2,1)S(1)}, bf16[2,320,384]{2,1,0:T(8,128)(2,1)}, u32[]{:S(2)}, u32[]{:S(2)}) %collective-permute-start.6) | collective-permute-done | bytes 491552 | tf_op jit(solution)/shard_map/ppermute | solution.py:197
  54.0 13.9 %collective-permute-start.4 = (f32[24,1536]{1,0:T(8,128)S(1)}, f32[24,1536]{1,0:T(8,128)S(1)}, u32[]{:S(2)}, u32[]{:S(2)}) collective-permute-start(f32[24,1536]{1,0:T(8,128)S(1)} %slice.346), channel_id=1, source_target_pairs={{0,2},{1,3},{2,0},{3,1},{4,6},{5,7},{6,4},{7,5},{8,10},{9,11},{10,... | collective-permute-start | bytes 442376 | tf_op jit(solution)/shard_map/ppermute | solution.py:197
  70.3 11.1 %collective-permute-done.4 = f32[24,1536]{1,0:T(8,128)S(1)} collective-permute-done((f32[24,1536]{1,0:T(8,128)S(1)}, f32[24,1536]{1,0:T(8,128)S(1)}, u32[]{:S(2)}, u32[]{:S(2)}) %collective-permute-start.4) | collective-permute-done | bytes 147488 | tf_op jit(solution)/shard_map/ppermute | solution.py:197
  82.3 3.0 fusion.62
  87.4 2.3 fusion.54
  112.6 3.9 collective-permute-done.10.refs_2_
  134.1 13.6 %attend.1 = (bf16[640,384]{1,0:T(8,128)(2,1)}, f32[640,384]{1,0:T(8,128)}) custom-call(bf16[640,384]{1,0:T(8,128)(2,1)} %get-tuple-element.158.q_ref, f32[2,1,1280]{2,1,0:T(1,128)} %broadcast_select_fusion.bias_ref, bf16[2,640,384]{2,1,0:T(8,128)(2,1)} %copy-done.8, bf16[2,640,384]{2,1,0:T(8,128)(2,1)} %collective-permute-done.9.refs_1_, ...), custom_call_target="tpu_custom_call" | custom-call | tf_op jit(solution)/shard_map/attend/pallas_call | solution.py:128
  149.6 2.4 convolution_convert_fusion
  152.2 3.0 collective-permute-start.14
  156.9 10.0 %collective-permute-done.14 = bf16[2,320,384]{2,1,0:T(8,128)(2,1)S(1)} collective-permute-done((bf16[2,320,384]{2,1,0:T(8,128)(2,1)S(1)}, bf16[2,320,384]{2,1,0:T(8,128)(2,1)S(1)}, u32[]{:S(2)}, u32[]{:S(2)}) %collective-permute-start.14) | collective-permute-done | bytes 491552 | tf_op jit(solution)/shard_map/ppermute | solution.py:197
  166.9 4.3 collective-permute-start.20
  171.2 7.2 %collective-permute-done.13 = bf16[2,320,384]{2,1,0:T(8,128)(2,1)S(1)} collective-permute-done((bf16[2,320,384]{2,1,0:T(8,128)(2,1)S(1)}, bf16[2,320,384]{2,1,0:T(8,128)(2,1)S(1)}, u32[]{:S(2)}, u32[]{:S(2)}) %collective-permute-start.13) | collective-permute-done | bytes 491552 | tf_op jit(solution)/shard_map/ppermute | solution.py:197
  178.4 20.1 %collective-permute-done.12 = bf16[2,320,384]{2,1,0:T(8,128)(2,1)S(1)} collective-permute-done((bf16[2,320,384]{2,1,0:T(8,128)(2,1)S(1)}, bf16[2,320,384]{2,1,0:T(8,128)(2,1)S(1)}, u32[]{:S(2)}, u32[]{:S(2)}) %collective-permute-start.12) | collective-permute-done | bytes 491552 | tf_op jit(solution)/shard_map/ppermute | solution.py:197
  200.2 23.4 %collective-permute-start.16 = (bf16[2,320,384]{2,1,0:T(8,128)(2,1)S(1)}, bf16[2,320,384]{2,1,0:T(8,128)(2,1)S(1)}, u32[]{:S(2)}, u32[]{:S(2)}) collective-permute-start(bf16[2,320,384]{2,1,0:T(8,128)(2,1)S(1)} %get-tuple-element.165), channel_id=1, source_target_pairs={{0,1},{1,2},{2,3},{3,0},{4,5},{5,6},{6,7},{7,4},{8,9},{9,10},{10,1... | collective-permute-start | bytes 1474568 | tf_op jit(solution)/shard_map/ppermute | solution.py:197
  228.4 16.7 %collective-permute-done.16 = bf16[2,320,384]{2,1,0:T(8,128)(2,1)S(1)} collective-permute-done((bf16[2,320,384]{2,1,0:T(8,128)(2,1)S(1)}, bf16[2,320,384]{2,1,0:T(8,128)(2,1)S(1)}, u32[]{:S(2)}, u32[]{:S(2)}) %collective-permute-start.16) | collective-permute-done | bytes 491552 | tf_op jit(solution)/shard_map/ppermute | solution.py:197
  245.2 2.6 collective-permute-done.17
  251.1 7.2 %fusion.29 = f32[2,256,1536]{2,1,0:T(8,128)} fusion(bf16[2,1536,1536]{2,1,0:T(8,128)(2,1)} %all-gather.9.cloned.1.call-done, f32[1536]{0:T(1024)} %add.674, f32[2,1536]{1,0:T(2,128)} %get-tuple-element.225, f32[2,1536]{1,0:T(2,128)} %get-tuple-element.226, f32[2,256]{1,0:T(2,128)} %add_rsqrt_fusion, f32[2,256]{1,0:T(2,128)} %copy-done.65, ...), kind=kOutput, calls=%fused_computation.70 | convolution fusion | flops 2421424128 | bytes 9474048 | tf_op jit(solution)/shard_map/snd,df->snf/dot_general | solution.py:310
  258.3 8.5 %fusion.183 = (f32[1536]{0:T(1024)}, bf16[2,256,1536]{2,1,0:T(8,128)(2,1)S(1)}) fusion(f32[2,256,1536]{2,1,0:T(8,128)} %fusion.29, bf16[2,1536,1536]{2,1,0:T(8,128)(2,1)} %all-gather.11.cloned.1.call-done, bf16[2,320,1536]{2,1,0:T(8,128)(2,1)} %constant_dynamic-update-slice_fusion.8, f32[2,1536]{1,0:T(2,128)} %get-tuple-element.222), kind=kOutput, calls=%fused_computation.420 | convolution fusion | flops 2434005504 | bytes 11028480 | tf_op jit(solution)/shard_map/sno,of->snf/dot_general | solution.py:310
  266.9 3.7 fusion.36
  273.2 2.8 fusion.184
  276.0 2.4 fusion.104
  280.5 9.0 %collective-permute-start.23 = (bf16[2,320,384]{2,1,0:T(8,128)(2,1)S(1)}, bf16[2,320,384]{2,1,0:T(8,128)(2,1)S(1)}, u32[]{:S(2)}, u32[]{:S(2)}) collective-permute-start(bf16[2,320,384]{2,1,0:T(8,128)(2,1)S(1)} %get-tuple-element.152), channel_id=1, source_target_pairs={{0,3},{1,0},{2,1},{3,2},{4,7},{5,4},{6,5},{7,6},{8,11},{9,8},{10,9... | collective-permute-start | bytes 1474568 | tf_op jit(solution)/shard_map/ppermute | solution.py:197
  290.7 10.3 %collective-permute-done.23 = bf16[2,320,384]{2,1,0:T(8,128)(2,1)S(1)} collective-permute-done((bf16[2,320,384]{2,1,0:T(8,128)(2,1)S(1)}, bf16[2,320,384]{2,1,0:T(8,128)(2,1)S(1)}, u32[]{:S(2)}, u32[]{:S(2)}) %collective-permute-start.23) | collective-permute-done | bytes 491552 | tf_op jit(solution)/shard_map/ppermute | solution.py:197
  301.1 11.8 %collective-permute-done.22 = bf16[2,320,384]{2,1,0:T(8,128)(2,1)S(1)} collective-permute-done((bf16[2,320,384]{2,1,0:T(8,128)(2,1)S(1)}, bf16[2,320,384]{2,1,0:T(8,128)(2,1)S(1)}, u32[]{:S(2)}, u32[]{:S(2)}) %collective-permute-start.22) | collective-permute-done | bytes 491552 | tf_op jit(solution)/shard_map/ppermute | solution.py:197
  312.9 18.7 %collective-permute-done.21 = bf16[2,320,384]{2,1,0:T(8,128)(2,1)S(1)} collective-permute-done((bf16[2,320,384]{2,1,0:T(8,128)(2,1)S(1)}, bf16[2,320,384]{2,1,0:T(8,128)(2,1)S(1)}, u32[]{:S(2)}, u32[]{:S(2)}) %collective-permute-start.21) | collective-permute-done | bytes 491552 | tf_op jit(solution)/shard_map/ppermute | solution.py:197
  332.8 3.2 collective-permute-start.25
  336.6 30.3 %collective-permute-done.24 = bf16[2,320,384]{2,1,0:T(8,128)(2,1)S(1)} collective-permute-done((bf16[2,320,384]{2,1,0:T(8,128)(2,1)S(1)}, bf16[2,320,384]{2,1,0:T(8,128)(2,1)S(1)}, u32[]{:S(2)}, u32[]{:S(2)}) %collective-permute-start.24) | collective-permute-done | bytes 491552 | tf_op jit(solution)/shard_map/ppermute | solution.py:197
  372.7 5.0 fusion.2
  377.7 4.8 fusion.6
  382.5 8.6 %pad_maximum_fusion = bf16[2,1536,1536]{2,1,0:T(8,128)(2,1)} fusion(bf16[1,1536,1536]{2,1,0:T(8,128)(2,1)} %fusion.2, bf16[1,1536,1536]{2,1,0:T(8,128)(2,1)} %fusion.6), kind=kLoop, calls=%fused_computation.2 | loop fusion | flops 4718592 | bytes 18874368 | tf_op jit(solution)/shard_map/stack | solution.py:484
  391.3 5.2 fusion.3
  396.5 6.1 fusion.7
  402.6 8.3 %pad_maximum_fusion.1 = bf16[2,1536,1536]{2,1,0:T(8,128)(2,1)} fusion(bf16[1,1536,1536]{2,1,0:T(8,128)(2,1)} %fusion.3, bf16[1,1536,1536]{2,1,0:T(8,128)(2,1)} %fusion.7), kind=kLoop, calls=%fused_computation.3 | loop fusion | flops 4718592 | bytes 18874368 | tf_op jit(solution)/shard_map/stack | solution.py:484
  412.8 2.7 fusion.71
  416.3 20.5 %attend_back.1 = (bf16[640,384]{1,0:T(8,128)(2,1)}, bf16[2,640,384]{2,1,0:T(8,128)(2,1)}, bf16[2,640,384]{2,1,0:T(8,128)(2,1)}, bf16[2,640,384]{2,1,0:T(8,128)(2,1)}, bf16[2,640,384]{2,1,0:T(8,128)(2,1)}) custom-call(bf16[640,384]{1,0:T(8,128)(2,1)} %get-tuple-element.158.q_ref, f32[2,1,1280]{2,1,0:T(1,128)} %broadcast_select_fusion.bias_ref, ...), custom_call_target="tpu_custom_call" | custom-call | tf_op jit(solution)/shard_map/attend_back/pallas_call | solution.py:145
  436.8 3.5 pad_maximum_fusion.4
  451.0 2.3 collective-permute-start.31
  453.3 4.1 fusion.15
  459.9 5.3 fusion.11
  467.3 8.9 %collective-permute-start.28 = (bf16[2,320,384]{2,1,0:T(8,128)(2,1)}, bf16[2,320,384]{2,1,0:T(8,128)(2,1)}, u32[]{:S(2)}, u32[]{:S(2)}) collective-permute-start(bf16[2,320,384]{2,1,0:T(8,128)(2,1)} %get-tuple-element.148), channel_id=1, source_target_pairs={{0,1},{1,2},{2,3},{3,0},{4,5},{5,6},{6,7},{7,4},{8,9},{9,10},{10,1... | collective-permute-start | bytes 1474568 | tf_op jit(solution)/shard_map/ppermute | solution.py:197
  476.2 2.1 collective-permute-start.27
  478.4 18.3 %collective-permute-done.31 = bf16[2,640,384]{2,1,0:T(8,128)(2,1)S(1)} collective-permute-done((bf16[2,640,384]{2,1,0:T(8,128)(2,1)S(1)}, bf16[2,640,384]{2,1,0:T(8,128)(2,1)S(1)}, u32[]{:S(2)}, u32[]{:S(2)}) %collective-permute-start.31) | collective-permute-done | bytes 983072 | tf_op jit(solution)/shard_map/ppermute | solution.py:200
  500.0 2.8 fusion.112
  503.5 4.9 fusion.44
  517.9 2.3 fusion.4
  520.3 2.4 fusion.5
  522.7 3.6 pad_maximum_fusion.2
  527.6 3.4 fusion.43
  532.0 2.2 collective-permute-start.36
  538.0 8.1 %collective-permute-start.34 = (bf16[2,320,384]{2,1,0:T(8,128)(2,1)S(1)}, bf16[2,320,384]{2,1,0:T(8,128)(2,1)S(1)}, u32[]{:S(2)}, u32[]{:S(2)}) collective-permute-start(bf16[2,320,384]{2,1,0:T(8,128)(2,1)S(1)} %get-tuple-element.146), channel_id=1, source_target_pairs={{0,3},{1,0},{2,1},{3,2},{4,7},{5,4},{6,5},{7,6},{8,11},{9,8},{10,9... | collective-permute-start | bytes 1474568 | tf_op jit(solution)/shard_map/ppermute | solution.py:197
  552.6 38.9 %collective-permute-done.38 = f32[8,1536]{1,0:T(8,128)S(1)} collective-permute-done((f32[8,1536]{1,0:T(8,128)S(1)}, f32[8,1536]{1,0:T(8,128)S(1)}, u32[]{:S(2)}, u32[]{:S(2)}) %collective-permute-start.38) | collective-permute-done | bytes 49184 | tf_op jit(solution)/shard_map/ppermute | solution.py:197
  594.8 2.1 multiply_reduce_fusion.3
  608.1 3.7 collective-permute-done.40
  617.1 2.4 collective-permute-done.45
  619.5 4.8 collective-permute-done.44
  632.3 2.2 fusion.77
  636.4 6.0 convolution_bitcast_fusion.2
  642.5 3.0 convert_element_type.321
  645.5 3.0 convert_element_type.324
  648.4 22.9 %reduce-scatter.5.cloned.1.call-done = bf16[2,192,1152]{2,1,0:T(8,128)(2,1)} async-done(((bf16[2,1536,1152]{2,1,0:T(8,128)(2,1)}), bf16[2,192,1152]{2,1,0:T(8,128)(2,1)}) %reduce-scatter.5.cloned.1.call-update) | async-done | bytes 884752 | tf_op jit(solution)/shard_map/reduce_scatter | solution.py:483
  (597 shorter events, 165.3 us)
Async XLA Ops:
  7.2 75.0 %all-gather.5.cloned.1.call-start = ((), (), s32[]{:S(2)}) async-start(), calls=%async_computation.4 | async-start | bytes 7962624 | tf_op jit(solution)/shard_map/all_gather | solution.py:242
  9.6 138.0 %all-gather.7.cloned.1.call-start = ((), (), s32[]{:S(2)}) async-start(), calls=%async_computation.5 | async-start | bytes 2654208 | tf_op jit(solution)/shard_map/all_gather | solution.py:242
  10.4 240.7 %all-gather.9.cloned.1.call-start = ((), (), s32[]{:S(2)}) async-start(), calls=%async_computation.6 | async-start | bytes 10616832 | tf_op jit(solution)/shard_map/all_gather | solution.py:242
  11.1 247.1 %all-gather.11.cloned.1.call-start = ((), (), s32[]{:S(2)}) async-start(), calls=%async_computation.7 | async-start | bytes 10616832 | tf_op jit(solution)/shard_map/all_gather | solution.py:242
  11.3 37.4 %collective-permute-start.6 = (bf16[2,320,384]{2,1,0:T(8,128)(2,1)S(1)}, bf16[2,320,384]{2,1,0:T(8,128)(2,1)}, u32[]{:S(2)}, u32[]{:S(2)}) collective-permute-start(bf16[2,320,384]{2,1,0:T(8,128)(2,1)S(1)} %constant_dynamic-update-slice_fusion.20), channel_id=1, source_target_pairs={{0,2},{1,3},{2,0},{3,1},{4,6},{5,7},{6,4},{7,5},{8,10},{9,11},{10,... | collective-permute-start | bytes 1474568 | tf_op jit(solution)/shard_map/ppermute | solution.py:197
  15.4 34.5 %collective-permute-start.7 = (bf16[2,320,384]{2,1,0:T(8,128)(2,1)S(1)}, bf16[2,320,384]{2,1,0:T(8,128)(2,1)}, u32[]{:S(2)}, u32[]{:S(2)}) collective-permute-start(bf16[2,320,384]{2,1,0:T(8,128)(2,1)S(1)} %constant_dynamic-update-slice_fusion.20), channel_id=1, source_target_pairs={{0,1},{1,2},{2,3},{3,0},{4,5},{5,6},{6,7},{7,4},{8,9},{9,10},{10,1... | collective-permute-start | bytes 1474568 | tf_op jit(solution)/shard_map/ppermute | solution.py:197
  17.0 34.1 %collective-permute-start.8 = (bf16[2,320,384]{2,1,0:T(8,128)(2,1)S(1)}, bf16[2,320,384]{2,1,0:T(8,128)(2,1)}, u32[]{:S(2)}, u32[]{:S(2)}) collective-permute-start(bf16[2,320,384]{2,1,0:T(8,128)(2,1)S(1)} %constant_dynamic-update-slice_fusion.20), channel_id=1, source_target_pairs={{0,3},{1,0},{2,1},{3,2},{4,7},{5,4},{6,5},{7,6},{8,11},{9,8},{10,9... | collective-permute-start | bytes 1474568 | tf_op jit(solution)/shard_map/ppermute | solution.py:197
  19.3 607.0 %reduce-scatter.7.cloned.1.call-start = ((), (), s32[]{:S(2)}) async-start(), calls=%async_computation.9 | async-start | bytes 2654208 | tf_op jit(solution)/shard_map/reduce_scatter | solution.py:483
  22.3 11.4 %collective-permute-start = (f32[28,1536]{1,0:T(8,128)S(1)}, f32[28,1536]{1,0:T(8,128)S(1)}, u32[]{:S(2)}, u32[]{:S(2)}) collective-permute-start(f32[28,1536]{1,0:T(8,128)S(1)} %pad_maximum_fusion.13), channel_id=1, source_target_pairs={{0,16},{16,0},{1,17},{17,1},{2,18},{18,2},{3,19},{19,3},{4,20},{20... | collective-permute-start | bytes 516104 | tf_op jit(solution)/shard_map/ppermute | solution.py:197
  33.7 1.5 collective-permute-start.1
  35.2 18.3 %collective-permute-start.2 = (f32[28,1536]{1,0:T(8,128)S(1)}, f32[28,1536]{1,0:T(8,128)S(1)}, u32[]{:S(2)}, u32[]{:S(2)}) collective-permute-start(f32[28,1536]{1,0:T(8,128)S(1)} %add.613), channel_id=1, source_target_pairs={{0,8},{4,12},{8,0},{12,4},{1,9},{5,13},{9,1},{13,5},{2,10},{6,14},... | collective-permute-start | bytes 516104 | tf_op jit(solution)/shard_map/ppermute | solution.py:200
  53.6 16.7 %collective-permute-start.5 = (f32[24,1536]{1,0:T(8,128)S(1)}, f32[24,1536]{1,0:T(8,128)S(1)}, u32[]{:S(2)}, u32[]{:S(2)}) collective-permute-start(f32[24,1536]{1,0:T(8,128)S(1)} %slice.346), channel_id=1, source_target_pairs={{0,3},{1,0},{2,1},{3,2},{4,7},{5,4},{6,5},{7,6},{8,11},{9,8},{10,9... | collective-permute-start | bytes 442376 | tf_op jit(solution)/shard_map/ppermute | solution.py:197
  54.0 27.3 %collective-permute-start.4 = (f32[24,1536]{1,0:T(8,128)S(1)}, f32[24,1536]{1,0:T(8,128)S(1)}, u32[]{:S(2)}, u32[]{:S(2)}) collective-permute-start(f32[24,1536]{1,0:T(8,128)S(1)} %slice.346), channel_id=1, source_target_pairs={{0,2},{1,3},{2,0},{3,1},{4,6},{5,7},{6,4},{7,5},{8,10},{9,11},{10,... | collective-permute-start | bytes 442376 | tf_op jit(solution)/shard_map/ppermute | solution.py:197
  67.9 13.4 %collective-permute-start.3 = (f32[24,1536]{1,0:T(8,128)S(1)}, f32[24,1536]{1,0:T(8,128)S(1)}, u32[]{:S(2)}, u32[]{:S(2)}) collective-permute-start(f32[24,1536]{1,0:T(8,128)S(1)} %slice.346), channel_id=1, source_target_pairs={{0,1},{1,2},{2,3},{3,0},{4,5},{5,6},{6,7},{7,4},{8,9},{9,10},{10,1... | collective-permute-start | bytes 442376 | tf_op jit(solution)/shard_map/ppermute | solution.py:197
  91.0 25.5 %collective-permute-start.10 = (bf16[2,640,384]{2,1,0:T(8,128)(2,1)S(1)}, bf16[2,640,384]{2,1,0:T(8,128)(2,1)}, u32[]{:S(2)}, u32[]{:S(2)}) collective-permute-start(bf16[2,640,384]{2,1,0:T(8,128)(2,1)S(1)} %pad_maximum_fusion.7.refs_0_), channel_id=1, source_target_pairs={{0,8},{4,12},{8,0},{12,4},{1,9},{5,13},{9,1},{13,5},{2,10},{6,14},... | collective-permute-start | bytes 2949128 | tf_op jit(solution)/shard_map/ppermute | solution.py:200
  107.0 116.7 %collective-permute-start.18 = (bf16[2,320,384]{2,1,0:T(8,128)(2,1)}, bf16[2,320,384]{2,1,0:T(8,128)(2,1)}, u32[]{:S(2)}, u32[]{:S(2)}) collective-permute-start(bf16[2,320,384]{2,1,0:T(8,128)(2,1)} %pad_maximum_fusion.9), channel_id=1, source_target_pairs={{0,2},{1,3},{2,0},{3,1},{4,6},{5,7},{6,4},{7,5},{8,10},{9,11},{10,... | collective-permute-start | bytes 1474568 | tf_op jit(solution)/shard_map/ppermute | solution.py:197
  107.0 118.6 %collective-permute-start.19 = (bf16[2,320,384]{2,1,0:T(8,128)(2,1)}, bf16[2,320,384]{2,1,0:T(8,128)(2,1)}, u32[]{:S(2)}, u32[]{:S(2)}) collective-permute-start(bf16[2,320,384]{2,1,0:T(8,128)(2,1)} %pad_maximum_fusion.9), channel_id=1, source_target_pairs={{0,1},{1,2},{2,3},{3,0},{4,5},{5,6},{6,7},{7,4},{8,9},{9,10},{10,1... | collective-permute-start | bytes 1474568 | tf_op jit(solution)/shard_map/ppermute | solution.py:197
  112.6 21.5 %collective-permute-start.9 = (bf16[2,640,384]{2,1,0:T(8,128)(2,1)S(1)}, bf16[2,640,384]{2,1,0:T(8,128)(2,1)}, u32[]{:S(2)}, u32[]{:S(2)}) collective-permute-start(bf16[2,640,384]{2,1,0:T(8,128)(2,1)S(1)} %pad_maximum_fusion.7.refs_0_), channel_id=1, source_target_pairs={{0,4},{4,0},{8,12},{12,8},{1,5},{5,1},{9,13},{13,9},{2,6},{6,2},{1... | collective-permute-start | bytes 2949128 | tf_op jit(solution)/shard_map/ppermute | solution.py:200
  116.5 17.6 %collective-permute-start.11 = (bf16[2,640,384]{2,1,0:T(8,128)(2,1)}, bf16[2,640,384]{2,1,0:T(8,128)(2,1)}, u32[]{:S(2)}, u32[]{:S(2)}) collective-permute-start(bf16[2,640,384]{2,1,0:T(8,128)(2,1)} %collective-permute-done.10.refs_2_), channel_id=1, source_target_pairs={{0,4},{4,0},{8,12},{12,8},{1,5},{5,1},{9,13},{13,9},{2,6},{6,2},{1... | collective-permute-start | bytes 2949128 | tf_op jit(solution)/shard_map/ppermute | solution.py:200
  152.2 46.5 %copy-start.24 = (bf16[2,64,384]{2,1,0:T(8,128)(2,1)S(1)}, bf16[2,64,384]{2,1,0:T(8,128)(2,1)}, u32[]{:S(2)}) copy-start(bf16[2,64,384]{2,1,0:T(8,128)(2,1)} %param.19) | copy-start | bytes 294916
  152.2 46.5 %copy-start.62 = (f32[2,64]{1,0:T(2,128)S(1)}, f32[2,64]{1,0:T(2,128)}, u32[]{:S(2)}) copy-start(f32[2,64]{1,0:T(2,128)} %copy-done.61) | copy-start | bytes 1540
  152.2 46.5 %copy-start.70 = (f32[384]{0:T(512)S(1)}, f32[384]{0:T(512)}, u32[]{:S(2)}) copy-start(f32[384]{0:T(512)} %add.664) | copy-start | bytes 4612
  152.2 14.7 %collective-permute-start.14 = (bf16[2,320,384]{2,1,0:T(8,128)(2,1)S(1)}, bf16[2,320,384]{2,1,0:T(8,128)(2,1)S(1)}, u32[]{:S(2)}, u32[]{:S(2)}) collective-permute-start(bf16[2,320,384]{2,1,0:T(8,128)(2,1)S(1)} %get-tuple-element.155), channel_id=1, source_target_pairs={{0,3},{1,0},{2,1},{3,2},{4,7},{5,4},{6,5},{7,6},{8,11},{9,8},{10,9... | collective-permute-start | bytes 1474568 | tf_op jit(solution)/shard_map/ppermute | solution.py:197
  155.2 23.1 %collective-permute-start.13 = (bf16[2,320,384]{2,1,0:T(8,128)(2,1)S(1)}, bf16[2,320,384]{2,1,0:T(8,128)(2,1)S(1)}, u32[]{:S(2)}, u32[]{:S(2)}) collective-permute-start(bf16[2,320,384]{2,1,0:T(8,128)(2,1)S(1)} %get-tuple-element.154), channel_id=1, source_target_pairs={{0,1},{1,2},{2,3},{3,0},{4,5},{5,6},{6,7},{7,4},{8,9},{9,10},{10,1... | collective-permute-start | bytes 1474568 | tf_op jit(solution)/shard_map/ppermute | solution.py:197
  155.2 43.2 %collective-permute-start.12 = (bf16[2,320,384]{2,1,0:T(8,128)(2,1)S(1)}, bf16[2,320,384]{2,1,0:T(8,128)(2,1)S(1)}, u32[]{:S(2)}, u32[]{:S(2)}) collective-permute-start(bf16[2,320,384]{2,1,0:T(8,128)(2,1)S(1)} %get-tuple-element.153), channel_id=1, source_target_pairs={{0,2},{1,3},{2,0},{3,1},{4,6},{5,7},{6,4},{7,5},{8,10},{9,11},{10,... | collective-permute-start | bytes 1474568 | tf_op jit(solution)/shard_map/ppermute | solution.py:197
  156.2 42.6 %copy-start.47 = (f32[2,384]{1,0:T(2,128)}, f32[2,384]{1,0:T(2,128)S(1)}, u32[]{:S(2)}) copy-start(f32[2,384]{1,0:T(2,128)S(1)} %get-tuple-element.218) | copy-start | bytes 9220
  156.9 42.0 %copy-start.68 = (f32[384]{0:T(512)S(1)}, f32[384]{0:T(512)}, u32[]{:S(2)}) copy-start(f32[384]{0:T(512)} %add.660) | copy-start | bytes 4612
  166.9 60.5 %collective-permute-start.20 = (bf16[2,320,384]{2,1,0:T(8,128)(2,1)}, bf16[2,320,384]{2,1,0:T(8,128)(2,1)S(1)}, u32[]{:S(2)}, u32[]{:S(2)}) collective-permute-start(bf16[2,320,384]{2,1,0:T(8,128)(2,1)} %pad_maximum_fusion.9), channel_id=1, source_target_pairs={{0,3},{1,0},{2,1},{3,2},{4,7},{5,4},{6,5},{7,6},{8,11},{9,8},{10,9... | collective-permute-start | bytes 1474568 | tf_op jit(solution)/shard_map/ppermute | solution.py:197
  199.3 29.0 %collective-permute-start.15 = (bf16[2,320,384]{2,1,0:T(8,128)(2,1)S(1)}, bf16[2,320,384]{2,1,0:T(8,128)(2,1)S(1)}, u32[]{:S(2)}, u32[]{:S(2)}) collective-permute-start(bf16[2,320,384]{2,1,0:T(8,128)(2,1)S(1)} %get-tuple-element.165), channel_id=1, source_target_pairs={{0,2},{1,3},{2,0},{3,1},{4,6},{5,7},{6,4},{7,5},{8,10},{9,11},{10,... | collective-permute-start | bytes 1474568 | tf_op jit(solution)/shard_map/ppermute | solution.py:197
  200.2 45.0 %collective-permute-start.16 = (bf16[2,320,384]{2,1,0:T(8,128)(2,1)S(1)}, bf16[2,320,384]{2,1,0:T(8,128)(2,1)S(1)}, u32[]{:S(2)}, u32[]{:S(2)}) collective-permute-start(bf16[2,320,384]{2,1,0:T(8,128)(2,1)S(1)} %get-tuple-element.165), channel_id=1, source_target_pairs={{0,1},{1,2},{2,3},{3,0},{4,5},{5,6},{6,7},{7,4},{8,9},{9,10},{10,1... | collective-permute-start | bytes 1474568 | tf_op jit(solution)/shard_map/ppermute | solution.py:197
  225.5 22.3 %collective-permute-start.17 = (bf16[2,320,384]{2,1,0:T(8,128)(2,1)S(1)}, bf16[2,320,384]{2,1,0:T(8,128)(2,1)S(1)}, u32[]{:S(2)}, u32[]{:S(2)}) collective-permute-start(bf16[2,320,384]{2,1,0:T(8,128)(2,1)S(1)} %get-tuple-element.165), channel_id=1, source_target_pairs={{0,3},{1,0},{2,1},{3,2},{4,7},{5,4},{6,5},{7,6},{8,11},{9,8},{10,9... | collective-permute-start | bytes 1474568 | tf_op jit(solution)/shard_map/ppermute | solution.py:197
  280.5 51.4 %copy-start.26 = (bf16[2,64,384]{2,1,0:T(8,128)(2,1)S(1)}, bf16[2,64,384]{2,1,0:T(8,128)(2,1)}, u32[]{:S(2)}) copy-start(bf16[2,64,384]{2,1,0:T(8,128)(2,1)} %param.35) | copy-start | bytes 294916
  280.5 20.6 %collective-permute-start.23 = (bf16[2,320,384]{2,1,0:T(8,128)(2,1)S(1)}, bf16[2,320,384]{2,1,0:T(8,128)(2,1)S(1)}, u32[]{:S(2)}, u32[]{:S(2)}) collective-permute-start(bf16[2,320,384]{2,1,0:T(8,128)(2,1)S(1)} %get-tuple-element.152), channel_id=1, source_target_pairs={{0,3},{1,0},{2,1},{3,2},{4,7},{5,4},{6,5},{7,6},{8,11},{9,8},{10,9... | collective-permute-start | bytes 1474568 | tf_op jit(solution)/shard_map/ppermute | solution.py:197
  289.5 23.4 %collective-permute-start.22 = (bf16[2,320,384]{2,1,0:T(8,128)(2,1)S(1)}, bf16[2,320,384]{2,1,0:T(8,128)(2,1)S(1)}, u32[]{:S(2)}, u32[]{:S(2)}) collective-permute-start(bf16[2,320,384]{2,1,0:T(8,128)(2,1)S(1)} %get-tuple-element.151), channel_id=1, source_target_pairs={{0,1},{1,2},{2,3},{3,0},{4,5},{5,6},{6,7},{7,4},{8,9},{9,10},{10,1... | collective-permute-start | bytes 1474568 | tf_op jit(solution)/shard_map/ppermute | solution.py:197
  289.5 42.4 %copy-start.48 = (f32[2,384]{1,0:T(2,128)S(1)}, f32[2,384]{1,0:T(2,128)}, u32[]{:S(2)}) copy-start(f32[2,384]{1,0:T(2,128)} %copy-done.47) | copy-start | bytes 9220
  289.5 42.1 %collective-permute-start.21 = (bf16[2,320,384]{2,1,0:T(8,128)(2,1)S(1)}, bf16[2,320,384]{2,1,0:T(8,128)(2,1)S(1)}, u32[]{:S(2)}, u32[]{:S(2)}) collective-permute-start(bf16[2,320,384]{2,1,0:T(8,128)(2,1)S(1)} %get-tuple-element.150), channel_id=1, source_target_pairs={{0,2},{1,3},{2,0},{3,1},{4,6},{5,7},{6,4},{7,5},{8,10},{9,11},{10,... | collective-permute-start | bytes 1474568 | tf_op jit(solution)/shard_map/ppermute | solution.py:197
  332.8 34.1 %collective-permute-start.24 = (bf16[2,320,384]{2,1,0:T(8,128)(2,1)S(1)}, bf16[2,320,384]{2,1,0:T(8,128)(2,1)S(1)}, u32[]{:S(2)}, u32[]{:S(2)}) collective-permute-start(bf16[2,320,384]{2,1,0:T(8,128)(2,1)S(1)} %get-tuple-element.163), channel_id=1, source_target_pairs={{0,2},{1,3},{2,0},{3,1},{4,6},{5,7},{6,4},{7,5},{8,10},{9,11},{10,... | collective-permute-start | bytes 1474568 | tf_op jit(solution)/shard_map/ppermute | solution.py:197
  332.8 34.2 %collective-permute-start.25 = (bf16[2,320,384]{2,1,0:T(8,128)(2,1)S(1)}, bf16[2,320,384]{2,1,0:T(8,128)(2,1)S(1)}, u32[]{:S(2)}, u32[]{:S(2)}) collective-permute-start(bf16[2,320,384]{2,1,0:T(8,128)(2,1)S(1)} %get-tuple-element.163), channel_id=1, source_target_pairs={{0,1},{1,2},{2,3},{3,0},{4,5},{5,6},{6,7},{7,4},{8,9},{9,10},{10,1... | collective-permute-start | bytes 1474568 | tf_op jit(solution)/shard_map/ppermute | solution.py:197
  336.0 32.5 %collective-permute-start.26 = (bf16[2,320,384]{2,1,0:T(8,128)(2,1)S(1)}, bf16[2,320,384]{2,1,0:T(8,128)(2,1)S(1)}, u32[]{:S(2)}, u32[]{:S(2)}) collective-permute-start(bf16[2,320,384]{2,1,0:T(8,128)(2,1)S(1)} %get-tuple-element.163), channel_id=1, source_target_pairs={{0,3},{1,0},{2,1},{3,2},{4,7},{5,4},{6,5},{7,6},{8,11},{9,8},{10,9... | collective-permute-start | bytes 1474568 | tf_op jit(solution)/shard_map/ppermute | solution.py:197
  372.5 269.9 %reduce-scatter.9.cloned.1.call-start = ((), (), s32[]{:S(2)}) async-start(), calls=%async_computation.10 | async-start | bytes 10616832 | tf_op jit(solution)/shard_map/reduce_scatter | solution.py:483
  391.1 254.4 %reduce-scatter.11.cloned.1.call-start = ((), (), s32[]{:S(2)}) async-start(), calls=%async_computation.11 | async-start | bytes 10616832 | tf_op jit(solution)/shard_map/reduce_scatter | solution.py:483
  410.9 260.4 %reduce-scatter.5.cloned.1.call-start = ((), (), s32[]{:S(2)}) async-start(), calls=%async_computation.8 | async-start | bytes 7962624 | tf_op jit(solution)/shard_map/reduce_scatter | solution.py:483
  440.3 8.9 %collective-permute-start.30 = (bf16[2,2,640,384]{3,2,1,0:T(8,128)(2,1)}, bf16[2,2,640,384]{3,2,1,0:T(8,128)(2,1)}, u32[]{:S(2)}, u32[]{:S(2)}) collective-permute-start(bf16[2,2,640,384]{3,2,1,0:T(8,128)(2,1)} %pad_maximum_fusion.4), channel_id=1, source_target_pairs={{0,4},{4,0},{8,12},{12,8},{1,5},{5,1},{9,13},{13,9},{2,6},{6,2},{1... | collective-permute-start | bytes 5898248 | tf_op jit(solution)/shard_map/ppermute | solution.py:200
  451.0 45.7 %collective-permute-start.31 = (bf16[2,640,384]{2,1,0:T(8,128)(2,1)S(1)}, bf16[2,640,384]{2,1,0:T(8,128)(2,1)S(1)}, u32[]{:S(2)}, u32[]{:S(2)}) collective-permute-start(bf16[2,640,384]{2,1,0:T(8,128)(2,1)S(1)} %fusion.63), channel_id=1, source_target_pairs={{0,8},{4,12},{8,0},{12,4},{1,9},{5,13},{9,1},{13,5},{2,10},{6,14},... | collective-permute-start | bytes 2949128 | tf_op jit(solution)/shard_map/ppermute | solution.py:200
  453.3 45.9 %slice-start.4 = ((s8[7077888]{0:T(1024)(128)(4,1)}), s8[4194304]{0:T(1024)(128)(4,1)S(1)}, s32[]{:S(2)}) async-start(s8[7077888]{0:T(1024)(128)(4,1)} %bitcast.289), calls=%async_computation.16 | async-start | bytes 8388608
  466.4 79.6 %collective-permute-start.29 = (bf16[2,320,384]{2,1,0:T(8,128)(2,1)}, bf16[2,320,384]{2,1,0:T(8,128)(2,1)}, u32[]{:S(2)}, u32[]{:S(2)}) collective-permute-start(bf16[2,320,384]{2,1,0:T(8,128)(2,1)} %get-tuple-element.149), channel_id=1, source_target_pairs={{0,3},{1,0},{2,1},{3,2},{4,7},{5,4},{6,5},{7,6},{8,11},{9,8},{10,9... | collective-permute-start | bytes 1474568 | tf_op jit(solution)/shard_map/ppermute | solution.py:197
  467.3 78.8 %collective-permute-start.28 = (bf16[2,320,384]{2,1,0:T(8,128)(2,1)}, bf16[2,320,384]{2,1,0:T(8,128)(2,1)}, u32[]{:S(2)}, u32[]{:S(2)}) collective-permute-start(bf16[2,320,384]{2,1,0:T(8,128)(2,1)} %get-tuple-element.148), channel_id=1, source_target_pairs={{0,1},{1,2},{2,3},{3,0},{4,5},{5,6},{6,7},{7,4},{8,9},{9,10},{10,1... | collective-permute-start | bytes 1474568 | tf_op jit(solution)/shard_map/ppermute | solution.py:197
  476.2 70.7 %collective-permute-start.27 = (bf16[2,320,384]{2,1,0:T(8,128)(2,1)}, bf16[2,320,384]{2,1,0:T(8,128)(2,1)}, u32[]{:S(2)}, u32[]{:S(2)}) collective-permute-start(bf16[2,320,384]{2,1,0:T(8,128)(2,1)} %get-tuple-element.147), channel_id=1, source_target_pairs={{0,2},{1,3},{2,0},{3,1},{4,6},{5,7},{6,4},{7,5},{8,10},{9,11},{10,... | collective-permute-start | bytes 1474568 | tf_op jit(solution)/shard_map/ppermute | solution.py:197
  516.4 14.7 %collective-permute-start.35 = (f32[9,1536]{1,0:T(8,128)}, f32[9,1536]{1,0:T(8,128)}, u32[]{:S(2)}, u32[]{:S(2)}) collective-permute-start(f32[9,1536]{1,0:T(8,128)} %dynamic-update-slice.11), channel_id=1, source_target_pairs={{0,4},{4,0},{8,12},{12,8},{1,5},{5,1},{9,13},{13,9},{2,6},{6,2},{1... | collective-permute-start | bytes 165896 | tf_op jit(solution)/shard_map/ppermute | solution.py:200
  532.0 5.7 collective-permute-start.36
  537.8 53.8 %copy-start.32 = (f32[9,1536]{1,0:T(8,128)}, f32[9,1536]{1,0:T(8,128)S(1)}, u32[]{:S(2)}) copy-start(f32[9,1536]{1,0:T(8,128)S(1)} %add.719) | copy-start | bytes 165892
  537.8 11.3 %collective-permute-start.39 = (f32[8,1536]{1,0:T(8,128)S(1)}, f32[8,1536]{1,0:T(8,128)S(1)}, u32[]{:S(2)}, u32[]{:S(2)}) collective-permute-start(f32[8,1536]{1,0:T(8,128)S(1)} %slice.410), channel_id=1, source_target_pairs={{0,3},{1,0},{2,1},{3,2},{4,7},{5,4},{6,5},{7,6},{8,11},{9,8},{10,9... | collective-permute-start | bytes 147464 | tf_op jit(solution)/shard_map/ppermute | solution.py:197
  538.0 54.3 %collective-permute-start.34 = (bf16[2,320,384]{2,1,0:T(8,128)(2,1)S(1)}, bf16[2,320,384]{2,1,0:T(8,128)(2,1)S(1)}, u32[]{:S(2)}, u32[]{:S(2)}) collective-permute-start(bf16[2,320,384]{2,1,0:T(8,128)(2,1)S(1)} %get-tuple-element.146), channel_id=1, source_target_pairs={{0,3},{1,0},{2,1},{3,2},{4,7},{5,4},{6,5},{7,6},{8,11},{9,8},{10,9... | collective-permute-start | bytes 1474568 | tf_op jit(solution)/shard_map/ppermute | solution.py:197
  546.1 46.2 %collective-permute-start.33 = (bf16[2,320,384]{2,1,0:T(8,128)(2,1)S(1)}, bf16[2,320,384]{2,1,0:T(8,128)(2,1)S(1)}, u32[]{:S(2)}, u32[]{:S(2)}) collective-permute-start(bf16[2,320,384]{2,1,0:T(8,128)(2,1)S(1)} %get-tuple-element.145), channel_id=1, source_target_pairs={{0,1},{1,2},{2,3},{3,0},{4,5},{5,6},{6,7},{7,4},{8,9},{9,10},{10,1... | collective-permute-start | bytes 1474568 | tf_op jit(solution)/shard_map/ppermute | solution.py:197
  546.1 46.8 %collective-permute-start.32 = (bf16[2,320,384]{2,1,0:T(8,128)(2,1)S(1)}, bf16[2,320,384]{2,1,0:T(8,128)(2,1)S(1)}, u32[]{:S(2)}, u32[]{:S(2)}) collective-permute-start(bf16[2,320,384]{2,1,0:T(8,128)(2,1)S(1)} %get-tuple-element.144), channel_id=1, source_target_pairs={{0,2},{1,3},{2,0},{3,1},{4,6},{5,7},{6,4},{7,5},{8,10},{9,11},{10,... | collective-permute-start | bytes 1474568 | tf_op jit(solution)/shard_map/ppermute | solution.py:197
  547.0 44.5 %collective-permute-start.38 = (f32[8,1536]{1,0:T(8,128)S(1)}, f32[8,1536]{1,0:T(8,128)S(1)}, u32[]{:S(2)}, u32[]{:S(2)}) collective-permute-start(f32[8,1536]{1,0:T(8,128)S(1)} %slice.410), channel_id=1, source_target_pairs={{0,2},{1,3},{2,0},{3,1},{4,6},{5,7},{6,4},{7,5},{8,10},{9,11},{10,... | collective-permute-start | bytes 147464 | tf_op jit(solution)/shard_map/ppermute | solution.py:197
  549.1 42.4 %collective-permute-start.37 = (f32[8,1536]{1,0:T(8,128)S(1)}, f32[8,1536]{1,0:T(8,128)S(1)}, u32[]{:S(2)}, u32[]{:S(2)}) collective-permute-start(f32[8,1536]{1,0:T(8,128)S(1)} %slice.410), channel_id=1, source_target_pairs={{0,1},{1,2},{2,3},{3,0},{4,5},{5,6},{6,7},{7,4},{8,9},{9,10},{10,1... | collective-permute-start | bytes 147464 | tf_op jit(solution)/shard_map/ppermute | solution.py:197
  605.7 2.2 collective-permute-start.41
  606.6 5.2 collective-permute-start.40
  608.0 6.0 collective-permute-start.42
  614.0 5.5 collective-permute-start.45
  615.4 8.9 %collective-permute-start.44 = (f32[16,1536]{1,0:T(8,128)S(1)}, f32[16,1536]{1,0:T(8,128)S(1)}, u32[]{:S(2)}, u32[]{:S(2)}) collective-permute-start(f32[16,1536]{1,0:T(8,128)S(1)} %slice.413), channel_id=1, source_target_pairs={{0,2},{1,3},{2,0},{3,1},{4,6},{5,7},{6,4},{7,5},{8,10},{9,11},{10,... | collective-permute-start | bytes 294920 | tf_op jit(solution)/shard_map/ppermute | solution.py:197
  615.4 8.9 %collective-permute-start.43 = (f32[16,1536]{1,0:T(8,128)S(1)}, f32[16,1536]{1,0:T(8,128)S(1)}, u32[]{:S(2)}, u32[]{:S(2)}) collective-permute-start(f32[16,1536]{1,0:T(8,128)S(1)} %slice.413), channel_id=1, source_target_pairs={{0,1},{1,2},{2,3},{3,0},{4,5},{5,6},{6,7},{7,4},{8,9},{9,10},{10,1... | collective-permute-start | bytes 294920 | tf_op jit(solution)/shard_map/ppermute | solution.py:197
  624.4 5.2 collective-permute-start.46
  (121 other events, 902.0 us)
Sparse Core Ops, SparseCore 0:
  10.5 53.6 all-gather.4
  66.0 29.0 all-gather.6
  97.0 64.9 all-gather.8
  163.8 58.6 all-gather.10
  372.7 49.9 reduce-scatter.6
  426.1 96.0 reduce-scatter.8
  525.7 76.6 reduce-scatter.10
  605.9 65.3 reduce-scatter.4
